TPU v7x, 256 devices: a whole 4x4x8 slice. The times are simulated.
256 devices in a mesh: row: 32 (over z_lo, y, core), col: 8 (over z_hi, x).
Axes of the slice: x: 4, y: 4, z: 8 (z_hi: 2, z_lo: 4; z = z_hi * 4 + z_lo), core: 2. Of those that a mesh axis runs over, the one named last changes fastest.
Arguments:
- weights: bfloat16 [8192, 32768], P('row', 'col'), may hold values from -6 to 6
- panel_first: float32 [256, 32768], P('row', 'col'), may hold values from -1 to 2, as said below
- panel_second: float32 [256, 32768], P('row', 'col'), may hold values from -1 to 2, as said below
- removed_first: int32 [512], P('col'), may hold values from -1 to 4095, as said below
- removed_second: int32 [512], P('col'), may hold values from -1 to 4095, as said below
Outputs:
- pruned: bfloat16 [8192, 32768], P('row', 'col')
Inputs may be any that keep to these rules, and one draw needn't show every extreme that they name: `removed_first`: in each list every owner's live slots come first; there are 256 live slots in all, at most 64 for one owner and exactly 64 for some owner; live values of one owner are distinct, and the two lists name no column twice. `removed_second`: same form as removed_first, with its own owners. `panel_first`: together with panel_second, its entries at the columns S1 and S2 are the rows of one symmetric positive definite matrix of order 2 * 256. `panel_second`: rows of the same inverse Hessian as panel_first, for the columns S2.
All inputs are finite; a program needn't handle non-finite values.
Results may differ from a plain program's by a relative error of at most 0.001.
Values may be sent and summed in bfloat16 or wider, within the bound.
No kernel may reach another device: no remote copies, remote signals or barrier semaphores. Data moves between devices by JAX's collectives and lax.ppermute only.
A program may use at most 64 MiB of HBM per device.

v0:
```python
import jax
import jax.numpy as jnp
from jax import lax
from jax.experimental import pallas as pl
from jax.experimental.pallas import tpu as pltpu
from jax.sharding import PartitionSpec as P


f32 = jnp.float32
bf16 = jnp.bfloat16
VMEM = pltpu.VMEM
MIB = 1 << 20
TOLERANCE = 3e-5
DOUBLINGS = 6
CODE_TOP = 32767.0
PARTS = 4
CORE, Y_ONE, Y_THREE, Z_ONE, Z_TWO, Z_THREE = 1, 2, 6, 8, 16, 24
X_ONE, X_THREE, Z_HALF = 1, 3, 4
OWNER_ORDER = (0, 4, 1, 5, 3, 7, 2, 6)
ENTRY_ORDER = tuple(c + y * 2 + z * 8 for c in (0, 1) for y in (0, 1, 3, 2) for z in range(4))
PANEL_ORDER = tuple(
    c + y * 2 + z * 8
    for c in (0, 1)
    for ys, zs in (((0, 1, 3, 2), (0, 1)), ((0, 3, 1, 2), (2, 3)))
    for y in ys
    for z in zs
)


def vmem_spec():
    return pl.BlockSpec(memory_space=VMEM)


def halves(value):
    high = value.astype(bf16)
    low = (value - high.astype(f32)).astype(bf16)
    return high, low


def dot(a, b):
    return jnp.dot(a, b, preferred_element_type=f32)


def product(a, b):
    a_high, a_low = halves(a)
    b_high, b_low = halves(b)
    return dot(a_high, b_high) + (dot(a_high, b_low) + dot(a_low, b_high))


def code_scale(exponent):
    return jnp.exp2(exponent.astype(f32) * 0.125)


def prepare_kernel(
    first_hbm,
    second_hbm,
    chosen_first_hbm,
    chosen_second_hbm,
    weights_hbm,
    codes_ref,
    slots_ref,
    mine_ref,
    panels_ref,
    chosen_first_ref,
    chosen_second_ref,
    weights_ref,
    onehot_ref,
    arrived,
):
    half, width = first_hbm.shape
    height = 2 * half
    part = width // PARTS
    moves = [
        (chosen_first_hbm, chosen_first_ref),
        (chosen_second_hbm, chosen_second_ref),
        (first_hbm, panels_ref.at[0:half]),
        (second_hbm, panels_ref.at[half:height]),
    ]
    for i in range(PARTS):
        columns = pl.ds(i * part, part)
        moves.append((weights_hbm.at[:, columns], weights_ref.at[:, columns]))
    copies = [
        pltpu.make_async_copy(source, target, arrived.at[i])
        for i, (source, target) in enumerate(moves)
    ]
    for copy in copies:
        copy.start()
    for copy in copies[0:4]:
        copy.wait()
    panels = panels_ref[...]
    size = jnp.abs(panels)
    most = jnp.maximum(jnp.max(size, axis=1, keepdims=True), 1e-30)
    exponent = jnp.ceil(jnp.log2(most) * 8.0).astype(jnp.int32)
    root = jnp.sqrt(size / code_scale(exponent))
    level = jnp.minimum(root * CODE_TOP + 0.5, CODE_TOP).astype(jnp.int32)
    codes_ref[:, 0:width] = jnp.where(panels < 0, -level, level).astype(jnp.int16)
    codes_ref[:, width:] = jnp.broadcast_to(exponent, (height, 128)).astype(jnp.int16)

    chosen = jnp.concatenate([chosen_first_ref[...], chosen_second_ref[...]], axis=1)
    column = lax.broadcasted_iota(jnp.int32, (width, chosen.shape[1]), 0)
    onehot_ref[...] = (column == chosen).astype(f32).astype(bf16)
    high = panels.astype(bf16)
    rest = panels - high.astype(f32)
    middle = rest.astype(bf16)
    low = (rest - middle.astype(f32)).astype(bf16)
    pieces = dot(jnp.concatenate([high, middle, low], axis=0), onehot_ref[...])
    slots_ref[0 : 3 * height, :] = pieces.astype(bf16)
    live = jnp.broadcast_to((chosen >= 0).astype(f32), (height, chosen.shape[1]))
    slots_ref[3 * height :, :] = live.astype(bf16)

    taken = None
    for i, copy in enumerate(copies[4:]):
        copy.wait()
        at = i * part
        share = dot(weights_ref[:, at : at + part], onehot_ref[at : at + part, :])
        taken = share if taken is None else taken + share
    mine_ref[...] = taken.astype(bf16)


def prepare(first, second, chosen_first, chosen_second, weights):
    height, width = 2 * first.shape[0], first.shape[1]
    rows = weights.shape[0]
    slots = 2 * chosen_first.shape[1]
    return pl.pallas_call(
        prepare_kernel,
        out_shape=(
            jax.ShapeDtypeStruct((height, width + 128), jnp.int16),
            jax.ShapeDtypeStruct((4 * height, slots), bf16),
            jax.ShapeDtypeStruct((rows, slots), bf16),
        ),
        in_specs=[pl.BlockSpec(memory_space=pltpu.HBM)] * 5,
        out_specs=(vmem_spec(),) * 3,
        scratch_shapes=[
            VMEM((height, width), f32),
            VMEM(chosen_first.shape, jnp.int32),
            VMEM(chosen_second.shape, jnp.int32),
            VMEM((rows, width), bf16),
            VMEM((width, slots), bf16),
            pltpu.SemaphoreType.DMA((4 + PARTS,)),
        ],
        name="prepare",
        compiler_params=pltpu.CompilerParams(vmem_limit_bytes=56360960),
    )(first, second, chosen_first, chosen_second, weights)


def mover(place, order):
    target = lax.broadcasted_iota(jnp.int32, (order, place.shape[1]), 0)
    return (target == place).astype(f32).astype(bf16)


def against(a, b):
    return lax.dot_general(a, b, (((1,), (1,)), ((), ())), preferred_element_type=f32)


def compact_kernel(near_ref, far_ref, entries_ref, places_ref):
    height, order = entries_ref.shape
    slots = near_ref.shape[1]
    half = slots // 2
    total = 4 * height
    per_device = height // 2
    me = lax.axis_index("col")
    lane = lax.broadcasted_iota(jnp.int32, (1, slots), 1)
    in_second = lane >= half
    slot = jnp.where(in_second, lane - half, lane)
    group = near_ref.shape[0] // total

    def block(index, start, stop):
        ref = near_ref if index < group else far_ref
        at = (index % group) * total
        return ref[at + start : at + stop, :]

    live = [block(i, 3 * height, total).astype(f32)[0:1, :] for i in range(len(OWNER_ORDER))]
    firsts = [jnp.sum(jnp.where(in_second, 0.0, x), axis=1, keepdims=True) for x in live]
    seconds = [jnp.sum(jnp.where(in_second, x, 0.0), axis=1, keepdims=True) for x in live]
    result = None
    for i, relative in enumerate(OWNER_ORDER):
        base_first = jnp.zeros((1, 1), f32)
        base_second = jnp.zeros((1, 1), f32)
        for j, other in enumerate(OWNER_ORDER):
            before = ((me ^ other) < (me ^ relative)).astype(f32)
            base_first = base_first + before * firsts[j]
            base_second = base_second + before * seconds[j]
        position = jnp.where(in_second, base_second, base_first).astype(jnp.int32) + slot
        place = (
            (position // per_device) * height
            + jnp.where(in_second, per_device, 0)
            + position % per_device
        )
        place = jnp.where(live[i] > 0.5, place, -1)
        places_ref[i : i + 1, :] = place
        share = against(block(i, 0, 3 * height), mover(place, order))
        result = share if result is None else result + share
    high = result[0:height, :]
    middle = result[height : 2 * height, :]
    entries_ref[...] = high + (middle + result[2 * height : 3 * height, :])


def compact(near, far, height, order):
    return pl.pallas_call(
        compact_kernel,
        out_shape=(
            jax.ShapeDtypeStruct((height, order), f32),
            jax.ShapeDtypeStruct((len(OWNER_ORDER), near.shape[1]), jnp.int32),
        ),
        in_specs=[vmem_spec()] * 2,
        out_specs=(vmem_spec(), vmem_spec()),
        name="compact",
        compiler_params=pltpu.CompilerParams(vmem_limit_bytes=8 * MIB),
    )(near, far)


def place_kernel(near_ref, far_ref, places_ref, columns_ref):
    rows, order = columns_ref.shape
    group = near_ref.shape[0] // rows
    result = None
    for i in range(len(OWNER_ORDER)):
        ref = near_ref if i < group else far_ref
        at = (i % group) * rows
        share = against(ref[at : at + rows, :], mover(places_ref[i : i + 1, :], order))
        result = share if result is None else result + share
    columns_ref[...] = result.astype(bf16)


def place(near, far, places, rows, order):
    return pl.pallas_call(
        place_kernel,
        out_shape=jax.ShapeDtypeStruct((rows, order), bf16),
        in_specs=[vmem_spec()] * 3,
        out_specs=vmem_spec(),
        name="place",
        compiler_params=pltpu.CompilerParams(vmem_limit_bytes=8 * MIB),
    )(near, far, places)


def solve_kernel(own_ref, sibling_ref, columns_ref, high_ref, low_ref, entries_ref, stacked, inverse):
    order = entries_ref.shape[0]
    rows = columns_ref.shape[0]
    me = lax.axis_index("row")
    height = order // len(ENTRY_ORDER)
    for i, relative in enumerate(ENTRY_ORDER):
        ref = own_ref if i < len(ENTRY_ORDER) // 2 else sibling_ref
        at = (i % (len(ENTRY_ORDER) // 2)) * height
        start = pl.multiple_of((me ^ relative) * height, height)
        entries_ref[pl.ds(start, height), :] = ref[at : at + height, :]
    row = lax.broadcasted_iota(jnp.int32, (order, order), 0)
    col = lax.broadcasted_iota(jnp.int32, (order, order), 1)
    entries = entries_ref[...]
    diagonal = jnp.where(row == col, entries, 0.0)
    scale_row = lax.rsqrt(jnp.sum(diagonal, axis=0, keepdims=True))
    scale_col = lax.rsqrt(jnp.sum(diagonal, axis=1, keepdims=True))
    unit = entries * scale_col * scale_row
    rest = jnp.where(row == col, 1.0 - unit, -unit)
    stacked[0:rows, :] = columns_ref[...].astype(f32) * scale_row
    stacked[rows:, :] = rest

    def bound():
        power = stacked[rows:, :]
        return jnp.sum(power * power)

    def going(state):
        count, left = state
        return jnp.logical_and(count < DOUBLINGS, jnp.logical_not(left < TOLERANCE))

    def double(state):
        count, _ = state
        power = stacked[rows:, :]
        result = product(stacked[...], power)
        stacked[0:rows, :] += result[0:rows, :]
        stacked[rows:, :] = result[rows:, :]
        return count + 1, bound()

    _, left = lax.while_loop(going, double, (jnp.int32(0), bound()))
    settled = left < TOLERANCE

    def finish(solved):
        index = lax.broadcasted_iota(jnp.int32, (1, order), 1)
        source = jnp.zeros((1, order), jnp.int32)
        for i, relative in enumerate(PANEL_ORDER):
            source = jnp.where(index // height == i, (me ^ relative) * height, source)
        arrange = (row == source + index % height).astype(f32).astype(bf16)
        high, low = halves(solved * (scale_row * (1.0 / (CODE_TOP * CODE_TOP))))
        high_ref[...] = dot(high, arrange).astype(bf16)
        low_ref[...] = dot(low, arrange).astype(bf16)

    @pl.when(settled)
    def _():
        solved = stacked[0:rows, :]
        finish(solved + product(solved, stacked[rows:, :]))

    @pl.when(jnp.logical_not(settled))
    def _():
        inverse[...] = entries_ref[...] * scale_col * scale_row

        def pivot(k, carry):
            lanes = lax.broadcasted_iota(jnp.int32, (1, order), 1)
            pivot_row = inverse[pl.ds(k, 1), :]
            head = jnp.sum(jnp.where(lanes == k, pivot_row, 0.0), axis=1, keepdims=True)
            pivot_row = jnp.where(lanes == k, 1.0, pivot_row) / head
            everything = inverse[...]
            column = jnp.sum(jnp.where(col == k, everything, 0.0), axis=1, keepdims=True)
            kept = jnp.where(col == k, 0.0, everything)
            inverse[...] = kept - column * pivot_row
            inverse[pl.ds(k, 1), :] = pivot_row
            return carry

        lax.fori_loop(0, order, pivot, 0)
        whole = entries_ref[...] * scale_col * scale_row
        wanted = columns_ref[...].astype(f32) * scale_row

        def exact(a, b):
            return jnp.dot(a, b, precision=lax.Precision.HIGHEST, preferred_element_type=f32)

        solved = exact(wanted, inverse[...])
        solved = solved + exact(wanted - exact(solved, whole), inverse[...])
        finish(solved)


def solve(own, sibling, columns):
    rows, order = columns.shape
    return pl.pallas_call(
        solve_kernel,
        out_shape=(jax.ShapeDtypeStruct((rows, order), bf16),) * 2,
        in_specs=[vmem_spec()] * 3,
        out_specs=(vmem_spec(), vmem_spec()),
        scratch_shapes=[
            VMEM((order, order), f32),
            VMEM((rows + order, order), f32),
            VMEM((order, order), f32),
        ],
        name="solve",
        compiler_params=pltpu.CompilerParams(vmem_limit_bytes=24 * MIB),
    )(own, sibling, columns)


def update_kernel(weights_ref, high_ref, low_ref, *rest):
    panels, out_ref = rest[:-1], rest[-1]
    tile = weights_ref.shape[1]
    width = panels[0].shape[1] - 128
    start = pl.multiple_of(pl.program_id(0) * tile, tile)
    pieces = []
    for ref in panels:
        scale = code_scale(ref[:, width:].astype(jnp.int32))[:, 0:1]
        code = ref[:, pl.ds(start, tile)].astype(jnp.int32).astype(f32)
        pieces.append(halves(code * jnp.abs(code) * scale))
    panel_high = jnp.concatenate([p[0] for p in pieces], axis=0)
    panel_low = jnp.concatenate([p[1] for p in pieces], axis=0)
    high = high_ref[...]
    change = dot(high, panel_high) + (dot(high, panel_low) + dot(low_ref[...], panel_high))
    out_ref[...] = (weights_ref[...].astype(f32) - change).astype(bf16)


def update(weights, high, low, panels):
    rows, width = weights.shape
    order = high.shape[1]
    tile = 512
    return pl.pallas_call(
        update_kernel,
        out_shape=jax.ShapeDtypeStruct((rows, width), bf16),
        grid=(width // tile,),
        in_specs=[
            pl.BlockSpec((rows, tile), lambda i: (0, i)),
            pl.BlockSpec((rows, order), lambda i: (0, 0)),
            pl.BlockSpec((rows, order), lambda i: (0, 0)),
        ]
        + [vmem_spec()] * len(panels),
        out_specs=pl.BlockSpec((rows, tile), lambda i: (0, i)),
        name="update",
        compiler_params=pltpu.CompilerParams(vmem_limit_bytes=24 * MIB),
    )(weights, high, low, *panels)


def swap(value, axis, relative):
    size = lax.axis_size(axis)
    return lax.ppermute(value, axis, [(i, i ^ relative) for i in range(size)])


def grow(value, axis, relative):
    return join(value, swap(value, axis, relative))


def join(*values):
    return lax.optimization_barrier(jnp.concatenate(values, axis=0))


def prune(weights, panel_first, panel_second, removed_first, removed_second):
    rows = weights.shape[0]
    height = 2 * panel_first.shape[0]
    order = height * lax.axis_size("row")
    chosen_first = removed_first[None, :]
    chosen_second = removed_second[None, :]
    codes, slots, mine = prepare(panel_first, panel_second, chosen_first, chosen_second, weights)

    near = grow(grow(slots, "col", Z_HALF), "col", X_ONE)
    far = swap(near, "col", X_THREE)
    entries, places = compact(near, far, height, order)
    entries = grow(entries, "row", Z_ONE)
    entries = grow(entries, "row", Z_TWO)
    entries = grow(entries, "row", Y_ONE)
    entries = grow(entries, "row", Y_THREE)
    sibling = swap(entries, "row", CORE)

    mine_near = grow(grow(mine, "col", Z_HALF), "col", X_ONE)
    mine_far = swap(mine_near, "col", X_THREE)
    columns = place(mine_near, mine_far, places, rows, order)

    even = grow(codes, "row", Z_ONE)
    even_one = swap(even, "row", Y_ONE)
    even_three = swap(even, "row", Y_THREE)
    even_two = swap(even_one, "row", Y_THREE)
    odd = join(swap(codes, "row", Z_TWO), swap(codes, "row", Z_THREE))
    odd_three = swap(odd, "row", Y_THREE)
    odd_one = swap(odd, "row", Y_ONE)
    odd_two = swap(odd_three, "row", Y_ONE)
    panels = [even, even_one, even_three, even_two, odd, odd_three, odd_one, odd_two]
    panels = panels + [swap(p, "row", CORE) for p in panels]

    high, low = solve(entries, sibling, columns)
    return update(weights, high, low, panels)


def solution(mesh):
    return jax.shard_map(
        prune,
        mesh=mesh,
        in_specs=(P("row", "col"), P("row", "col"), P("row", "col"), P("col"), P("col")),
        out_specs=P("row", "col"),
        check_vma=False,
    )
```

profile of v0, /device:TPU:1, one launch (start us, length us, event | category | flops | bytes accessed | tf_op | source)
XLA Modules:
  0.0 95.2 jit_solution(18098563586103857760)
XLA Ops:
  0.0 0.7 copy-done.1
  0.7 0.7 copy-done.2
  1.3 3.3 %prepare.1 = (s16[16,4224]{1,0:T(8,128)(2,1)}, bf16[64,128]{1,0:T(8,128)(2,1)S(1)}, bf16[256,128]{1,0:T(8,128)(2,1)S(1)}) custom-call(f32[8,4096]{1,0:T(8,128)} %first_hbm.1, f32[8,4096]{1,0:T(8,128)} %second_hbm.1, s32[1,64]{1,0:T(1,128)S(1)} %bitcast.2, s32[1,64]{1,0:T(1,128)S(1)} %bitcast.3, bf16[256,4096]{1,0:T(8,128)(2,1)} %weights_ref.1), custom_call_target="tpu_custom_call" | custom-call | tf_op jit(solution)/shard_map/prepare/pallas_call | solution.py:124
  4.6 7.8 %collective-permute-start = (bf16[64,128]{1,0:T(8,128)(2,1)S(1)}, bf16[64,128]{1,0:T(8,128)(2,1)S(1)}, u32[]{:S(2)}, u32[]{:S(2)}) collective-permute-start(bf16[64,128]{1,0:T(8,128)(2,1)S(1)} %get-tuple-element.12), channel_id=1, source_target_pairs={{0,4},{1,5},{2,6},{3,7},{4,0},{5,1},{6,2},{7,3},{8,12},{9,13},{10,... | collective-permute-start | bytes 49160 | tf_op jit(solution)/shard_map/ppermute | solution.py:374
  12.5 1.1 %collective-permute-done = bf16[64,128]{1,0:T(8,128)(2,1)S(1)} collective-permute-done((bf16[64,128]{1,0:T(8,128)(2,1)S(1)}, bf16[64,128]{1,0:T(8,128)(2,1)S(1)}, u32[]{:S(2)}, u32[]{:S(2)}) %collective-permute-start) | collective-permute-done | bytes 16416 | tf_op jit(solution)/shard_map/ppermute | solution.py:374
  13.6 1.2 %collective-permute-start.1 = (bf16[128,128]{1,0:T(8,128)(2,1)S(1)}, bf16[128,128]{1,0:T(8,128)(2,1)S(1)}, u32[]{:S(2)}, u32[]{:S(2)}) collective-permute-start(bf16[128,128]{1,0:T(8,128)(2,1)S(1)} %pad_maximum_fusion.7), channel_id=1, source_target_pairs={{0,1},{1,0},{2,3},{3,2},{4,5},{5,4},{6,7},{7,6},{8,9},{9,8},{10,11... | collective-permute-start | bytes 98312 | tf_op jit(solution)/shard_map/ppermute | solution.py:374
  14.8 1.6 %collective-permute-done.1 = bf16[128,128]{1,0:T(8,128)(2,1)S(1)} collective-permute-done((bf16[128,128]{1,0:T(8,128)(2,1)S(1)}, bf16[128,128]{1,0:T(8,128)(2,1)S(1)}, u32[]{:S(2)}, u32[]{:S(2)}) %collective-permute-start.1) | collective-permute-done | bytes 32800 | tf_op jit(solution)/shard_map/ppermute | solution.py:374
  16.4 2.5 %collective-permute-start.2 = (bf16[256,128]{1,0:T(8,128)(2,1)S(1)}, bf16[256,128]{1,0:T(8,128)(2,1)S(1)}, u32[]{:S(2)}, u32[]{:S(2)}) collective-permute-start(bf16[256,128]{1,0:T(8,128)(2,1)S(1)} %pad_maximum_fusion.5.near_ref), channel_id=1, source_target_pairs={{0,3},{1,2},{2,1},{3,0},{4,7},{5,6},{6,5},{7,4},{8,11},{9,10},{10,... | collective-permute-start | bytes 196616 | tf_op jit(solution)/shard_map/ppermute | solution.py:374
  18.8 1.9 %collective-permute-done.2.far_ref = bf16[256,128]{1,0:T(8,128)(2,1)S(1)} collective-permute-done((bf16[256,128]{1,0:T(8,128)(2,1)S(1)}, bf16[256,128]{1,0:T(8,128)(2,1)S(1)}, u32[]{:S(2)}, u32[]{:S(2)}) %collective-permute-start.2) | collective-permute-done | bytes 65568 | tf_op jit(solution)/shard_map/ppermute | solution.py:374
  21.3 0.8 collective-permute-start.3
  22.0 2.1 %collective-permute-start.16 = (s16[16,4224]{1,0:T(8,128)(2,1)}, s16[16,4224]{1,0:T(8,128)(2,1)S(1)}, u32[]{:S(2)}, u32[]{:S(2)}) collective-permute-start(s16[16,4224]{1,0:T(8,128)(2,1)} %get-tuple-element.18), channel_id=1, source_target_pairs={{0,192},{8,200},{16,208},{24,216},{32,224},{40,232},{48,240},{56,2... | collective-permute-start | bytes 405512 | tf_op jit(solution)/shard_map/ppermute | solution.py:374
  24.4 1.2 %collective-permute-start.11 = (s16[16,4224]{1,0:T(8,128)(2,1)}, s16[16,4224]{1,0:T(8,128)(2,1)S(1)}, u32[]{:S(2)}, u32[]{:S(2)}) collective-permute-start(s16[16,4224]{1,0:T(8,128)(2,1)} %get-tuple-element.18), channel_id=1, source_target_pairs={{0,64},{8,72},{16,80},{24,88},{32,96},{40,104},{48,112},{56,120},{... | collective-permute-start | bytes 405512 | tf_op jit(solution)/shard_map/ppermute | solution.py:374
  25.6 5.4 %collective-permute-start.8 = (bf16[256,128]{1,0:T(8,128)(2,1)S(1)}, bf16[256,128]{1,0:T(8,128)(2,1)S(1)}, u32[]{:S(2)}, u32[]{:S(2)}) collective-permute-start(bf16[256,128]{1,0:T(8,128)(2,1)S(1)} %get-tuple-element.14), channel_id=1, source_target_pairs={{0,4},{1,5},{2,6},{3,7},{4,0},{5,1},{6,2},{7,3},{8,12},{9,13},{10,... | collective-permute-start | bytes 196616 | tf_op jit(solution)/shard_map/ppermute | solution.py:374
  31.5 4.9 %collective-permute-done.8 = bf16[256,128]{1,0:T(8,128)(2,1)S(1)} collective-permute-done((bf16[256,128]{1,0:T(8,128)(2,1)S(1)}, bf16[256,128]{1,0:T(8,128)(2,1)S(1)}, u32[]{:S(2)}, u32[]{:S(2)}) %collective-permute-start.8) | collective-permute-done | bytes 65568 | tf_op jit(solution)/shard_map/ppermute | solution.py:374
  36.5 2.7 %collective-permute-done.4 = f32[32,512]{1,0:T(8,128)S(1)} collective-permute-done((f32[32,512]{1,0:T(8,128)S(1)}, f32[32,512]{1,0:T(8,128)S(1)}, u32[]{:S(2)}, u32[]{:S(2)}) %collective-permute-start.4) | collective-permute-done | bytes 65568 | tf_op jit(solution)/shard_map/ppermute | solution.py:374
  39.2 1.4 %collective-permute-start.5 = (f32[64,512]{1,0:T(8,128)S(1)}, f32[64,512]{1,0:T(8,128)S(1)}, u32[]{:S(2)}, u32[]{:S(2)}) collective-permute-start(f32[64,512]{1,0:T(8,128)S(1)} %pad_maximum_fusion.3), channel_id=1, source_target_pairs={{0,16},{8,24},{16,0},{24,8},{32,48},{40,56},{48,32},{56,40},{64,80... | collective-permute-start | bytes 393224 | tf_op jit(solution)/shard_map/ppermute | solution.py:374
  40.6 0.9 pad_add_fusion.rest_0_
  41.5 5.1 %collective-permute-start.20 = (s16[32,4224]{1,0:T(8,128)(2,1)S(1)}, s16[32,4224]{1,0:T(8,128)(2,1)S(1)}, u32[]{:S(2)}, u32[]{:S(2)}) collective-permute-start(s16[32,4224]{1,0:T(8,128)(2,1)S(1)} %pad_add_fusion.rest_0_), channel_id=1, source_target_pairs={{0,8},{8,0},{16,24},{24,16},{32,40},{40,32},{48,56},{56,48},{64,72... | collective-permute-start | bytes 811016 | tf_op jit(solution)/shard_map/ppermute | solution.py:374
  46.6 1.9 %collective-permute-start.13 = (s16[32,4224]{1,0:T(8,128)(2,1)S(1)}, s16[32,4224]{1,0:T(8,128)(2,1)S(1)}, u32[]{:S(2)}, u32[]{:S(2)}) collective-permute-start(s16[32,4224]{1,0:T(8,128)(2,1)S(1)} %pad_add_fusion.rest_0_), channel_id=1, source_target_pairs={{0,48},{8,56},{16,32},{24,40},{32,16},{40,24},{48,0},{56,8},{64,11... | collective-permute-start | bytes 811016 | tf_op jit(solution)/shard_map/ppermute | solution.py:374
  49.0 0.6 collective-permute-start.6
  49.7 3.8 %collective-permute-start.24 = (s16[32,4224]{1,0:T(8,128)(2,1)S(1)}, s16[32,4224]{1,0:T(8,128)(2,1)S(1)}, u32[]{:S(2)}, u32[]{:S(2)}) collective-permute-start(s16[32,4224]{1,0:T(8,128)(2,1)S(1)} %pad_add_fusion.1.rest_4_), channel_id=1, source_target_pairs={{0,8},{8,0},{16,24},{24,16},{32,40},{40,32},{48,56},{56,48},{64,72... | collective-permute-start | bytes 811016 | tf_op jit(solution)/shard_map/ppermute | solution.py:374
  53.4 1.9 %collective-permute-start.17 = (s16[32,4224]{1,0:T(8,128)(2,1)S(1)}, s16[32,4224]{1,0:T(8,128)(2,1)S(1)}, u32[]{:S(2)}, u32[]{:S(2)}) collective-permute-start(s16[32,4224]{1,0:T(8,128)(2,1)S(1)} %pad_add_fusion.1.rest_4_), channel_id=1, source_target_pairs={{0,48},{8,56},{16,32},{24,40},{32,16},{40,24},{48,0},{56,8},{64,11... | collective-permute-start | bytes 811016 | tf_op jit(solution)/shard_map/ppermute | solution.py:374
  55.3 3.8 %collective-permute-done.6 = f32[128,512]{1,0:T(8,128)S(1)} collective-permute-done((f32[128,512]{1,0:T(8,128)S(1)}, f32[128,512]{1,0:T(8,128)S(1)}, u32[]{:S(2)}, u32[]{:S(2)}) %collective-permute-start.6) | collective-permute-done | bytes 262176 | tf_op jit(solution)/shard_map/ppermute | solution.py:374
  59.1 6.3 %collective-permute-start.7 = (f32[256,512]{1,0:T(8,128)S(1)}, f32[256,512]{1,0:T(8,128)S(1)}, u32[]{:S(2)}, u32[]{:S(2)}) collective-permute-start(f32[256,512]{1,0:T(8,128)S(1)} %pad_maximum_fusion.own_ref), channel_id=1, source_target_pairs={{0,8},{8,0},{16,24},{24,16},{32,40},{40,32},{48,56},{56,48},{64,72... | collective-permute-start | bytes 1572872 | tf_op jit(solution)/shard_map/ppermute | solution.py:374
  65.6 2.0 %collective-permute-start.14 = (s16[32,4224]{1,0:T(8,128)(2,1)S(1)}, s16[32,4224]{1,0:T(8,128)(2,1)S(1)}, u32[]{:S(2)}, u32[]{:S(2)}) collective-permute-start(s16[32,4224]{1,0:T(8,128)(2,1)S(1)} %collective-permute-done.12.rest_1_), channel_id=1, source_target_pairs={{0,48},{8,56},{16,32},{24,40},{32,16},{40,24},{48,0},{56,8},{64,11... | collective-permute-start | bytes 811016 | tf_op jit(solution)/shard_map/ppermute | solution.py:374
  67.6 1.1 %collective-permute-start.19 = (s16[32,4224]{1,0:T(8,128)(2,1)S(1)}, s16[32,4224]{1,0:T(8,128)(2,1)S(1)}, u32[]{:S(2)}, u32[]{:S(2)}) collective-permute-start(s16[32,4224]{1,0:T(8,128)(2,1)S(1)} %collective-permute-done.17.rest_5_), channel_id=1, source_target_pairs={{0,16},{8,24},{16,0},{24,8},{32,48},{40,56},{48,32},{56,40},{64,80... | collective-permute-start | bytes 811016 | tf_op jit(solution)/shard_map/ppermute | solution.py:374
  68.7 2.3 %collective-permute-start.10 = (bf16[1024,128]{1,0:T(8,128)(2,1)S(1)}, bf16[1024,128]{1,0:T(8,128)(2,1)S(1)}, u32[]{:S(2)}, u32[]{:S(2)}) collective-permute-start(bf16[1024,128]{1,0:T(8,128)(2,1)S(1)} %pad_maximum_fusion.2.near_ref), channel_id=1, source_target_pairs={{0,3},{1,2},{2,1},{3,0},{4,7},{5,6},{6,5},{7,4},{8,11},{9,10},{10,... | collective-permute-start | bytes 786440 | tf_op jit(solution)/shard_map/ppermute | solution.py:374
  71.0 4.3 %collective-permute-done.10.far_ref = bf16[1024,128]{1,0:T(8,128)(2,1)S(1)} collective-permute-done((bf16[1024,128]{1,0:T(8,128)(2,1)S(1)}, bf16[1024,128]{1,0:T(8,128)(2,1)S(1)}, u32[]{:S(2)}, u32[]{:S(2)}) %collective-permute-start.10) | collective-permute-done | bytes 262176 | tf_op jit(solution)/shard_map/ppermute | solution.py:374
  75.3 4.8 %collective-permute-start.21 = (s16[32,4224]{1,0:T(8,128)(2,1)S(1)}, s16[32,4224]{1,0:T(8,128)(2,1)S(1)}, u32[]{:S(2)}, u32[]{:S(2)}) collective-permute-start(s16[32,4224]{1,0:T(8,128)(2,1)S(1)} %collective-permute-done.12.rest_1_), channel_id=1, source_target_pairs={{0,8},{8,0},{16,24},{24,16},{32,40},{40,32},{48,56},{56,48},{64,72... | collective-permute-start | bytes 811016 | tf_op jit(solution)/shard_map/ppermute | solution.py:374
  81.1 0.7 place.1.columns_ref
  81.8 6.5 %solve.1 = (bf16[256,512]{1,0:T(8,128)(2,1)S(1)}, bf16[256,512]{1,0:T(8,128)(2,1)S(1)}) custom-call(f32[256,512]{1,0:T(8,128)S(1)} %pad_maximum_fusion.own_ref, f32[256,512]{1,0:T(8,128)S(1)} %collective-permute-done.7.sibling_ref, bf16[256,512]{1,0:T(8,128)(2,1)S(1)} %place.1.columns_ref), custom_call_target="tpu_custom_call" | custom-call | tf_op jit(solution)/shard_map/solve/pallas_call | solution.py:320
  88.4 6.8 %update.1 = bf16[256,4096]{1,0:T(8,128)(2,1)} custom-call(bf16[256,4096]{1,0:T(8,128)(2,1)S(1)} %copy-done, bf16[256,512]{1,0:T(8,128)(2,1)S(1)} %get-tuple-element.16.high_ref, bf16[256,512]{1,0:T(8,128)(2,1)S(1)} %get-tuple-element.17.low_ref, s16[32,4224]{1,0:T(8,128)(2,1)S(1)} %pad_add_fusion.rest_0_, ...), custom_call_target="tpu_custom_call" | custom-call | tf_op jit(solution)/shard_map/update/pallas_call | solution.py:356
  (45 shorter events, 3.3 us)
Async XLA Ops:
  0.0 0.7 copy-start.1
  0.7 0.7 copy-start.2
  4.6 8.9 %collective-permute-start = (bf16[64,128]{1,0:T(8,128)(2,1)S(1)}, bf16[64,128]{1,0:T(8,128)(2,1)S(1)}, u32[]{:S(2)}, u32[]{:S(2)}) collective-permute-start(bf16[64,128]{1,0:T(8,128)(2,1)S(1)} %get-tuple-element.12), channel_id=1, source_target_pairs={{0,4},{1,5},{2,6},{3,7},{4,0},{5,1},{6,2},{7,3},{8,12},{9,13},{10,... | collective-permute-start | bytes 49160 | tf_op jit(solution)/shard_map/ppermute | solution.py:374
  13.6 2.8 %collective-permute-start.1 = (bf16[128,128]{1,0:T(8,128)(2,1)S(1)}, bf16[128,128]{1,0:T(8,128)(2,1)S(1)}, u32[]{:S(2)}, u32[]{:S(2)}) collective-permute-start(bf16[128,128]{1,0:T(8,128)(2,1)S(1)} %pad_maximum_fusion.7), channel_id=1, source_target_pairs={{0,1},{1,0},{2,3},{3,2},{4,5},{5,4},{6,7},{7,6},{8,9},{9,8},{10,11... | collective-permute-start | bytes 98312 | tf_op jit(solution)/shard_map/ppermute | solution.py:374
  16.4 4.3 %collective-permute-start.2 = (bf16[256,128]{1,0:T(8,128)(2,1)S(1)}, bf16[256,128]{1,0:T(8,128)(2,1)S(1)}, u32[]{:S(2)}, u32[]{:S(2)}) collective-permute-start(bf16[256,128]{1,0:T(8,128)(2,1)S(1)} %pad_maximum_fusion.5.near_ref), channel_id=1, source_target_pairs={{0,3},{1,2},{2,1},{3,0},{4,7},{5,6},{6,5},{7,4},{8,11},{9,10},{10,... | collective-permute-start | bytes 196616 | tf_op jit(solution)/shard_map/ppermute | solution.py:374
  21.3 9.7 %collective-permute-start.3 = (f32[16,512]{1,0:T(8,128)S(1)}, f32[16,512]{1,0:T(8,128)S(1)}, u32[]{:S(2)}, u32[]{:S(2)}) collective-permute-start(f32[16,512]{1,0:T(8,128)S(1)} %get-tuple-element.13), channel_id=1, source_target_pairs={{0,64},{8,72},{16,80},{24,88},{32,96},{40,104},{48,112},{56,120},{... | collective-permute-start | bytes 98312 | tf_op jit(solution)/shard_map/ppermute | solution.py:374
  22.0 26.5 %collective-permute-start.16 = (s16[16,4224]{1,0:T(8,128)(2,1)}, s16[16,4224]{1,0:T(8,128)(2,1)S(1)}, u32[]{:S(2)}, u32[]{:S(2)}) collective-permute-start(s16[16,4224]{1,0:T(8,128)(2,1)} %get-tuple-element.18), channel_id=1, source_target_pairs={{0,192},{8,200},{16,208},{24,216},{32,224},{40,232},{48,240},{56,2... | collective-permute-start | bytes 405512 | tf_op jit(solution)/shard_map/ppermute | solution.py:374
  24.2 24.9 %collective-permute-start.15 = (s16[16,4224]{1,0:T(8,128)(2,1)}, s16[16,4224]{1,0:T(8,128)(2,1)S(1)}, u32[]{:S(2)}, u32[]{:S(2)}) collective-permute-start(s16[16,4224]{1,0:T(8,128)(2,1)} %get-tuple-element.18), channel_id=1, source_target_pairs={{0,128},{8,136},{16,144},{24,152},{32,160},{40,168},{48,176},{56,1... | collective-permute-start | bytes 405512 | tf_op jit(solution)/shard_map/ppermute | solution.py:374
  24.4 16.2 %collective-permute-start.11 = (s16[16,4224]{1,0:T(8,128)(2,1)}, s16[16,4224]{1,0:T(8,128)(2,1)S(1)}, u32[]{:S(2)}, u32[]{:S(2)}) collective-permute-start(s16[16,4224]{1,0:T(8,128)(2,1)} %get-tuple-element.18), channel_id=1, source_target_pairs={{0,64},{8,72},{16,80},{24,88},{32,96},{40,104},{48,112},{56,120},{... | collective-permute-start | bytes 405512 | tf_op jit(solution)/shard_map/ppermute | solution.py:374
  25.6 10.8 %collective-permute-start.8 = (bf16[256,128]{1,0:T(8,128)(2,1)S(1)}, bf16[256,128]{1,0:T(8,128)(2,1)S(1)}, u32[]{:S(2)}, u32[]{:S(2)}) collective-permute-start(bf16[256,128]{1,0:T(8,128)(2,1)S(1)} %get-tuple-element.14), channel_id=1, source_target_pairs={{0,4},{1,5},{2,6},{3,7},{4,0},{5,1},{6,2},{7,3},{8,12},{9,13},{10,... | collective-permute-start | bytes 196616 | tf_op jit(solution)/shard_map/ppermute | solution.py:374
  31.0 8.3 %collective-permute-start.4 = (f32[32,512]{1,0:T(8,128)S(1)}, f32[32,512]{1,0:T(8,128)S(1)}, u32[]{:S(2)}, u32[]{:S(2)}) collective-permute-start(f32[32,512]{1,0:T(8,128)S(1)} %pad_maximum_fusion.6), channel_id=1, source_target_pairs={{0,128},{8,136},{16,144},{24,152},{32,160},{40,168},{48,176},{56,1... | collective-permute-start | bytes 196616 | tf_op jit(solution)/shard_map/ppermute | solution.py:374
  36.4 13.3 %collective-permute-start.9 = (bf16[512,128]{1,0:T(8,128)(2,1)S(1)}, bf16[512,128]{1,0:T(8,128)(2,1)S(1)}, u32[]{:S(2)}, u32[]{:S(2)}) collective-permute-start(bf16[512,128]{1,0:T(8,128)(2,1)S(1)} %pad_maximum_fusion.4), channel_id=1, source_target_pairs={{0,1},{1,0},{2,3},{3,2},{4,5},{5,4},{6,7},{7,6},{8,9},{9,8},{10,11... | collective-permute-start | bytes 393224 | tf_op jit(solution)/shard_map/ppermute | solution.py:374
  39.2 7.4 %collective-permute-start.5 = (f32[64,512]{1,0:T(8,128)S(1)}, f32[64,512]{1,0:T(8,128)S(1)}, u32[]{:S(2)}, u32[]{:S(2)}) collective-permute-start(f32[64,512]{1,0:T(8,128)S(1)} %pad_maximum_fusion.3), channel_id=1, source_target_pairs={{0,16},{8,24},{16,0},{24,8},{32,48},{40,56},{48,32},{56,40},{64,80... | collective-permute-start | bytes 393224 | tf_op jit(solution)/shard_map/ppermute | solution.py:374
  41.5 11.9 %collective-permute-start.20 = (s16[32,4224]{1,0:T(8,128)(2,1)S(1)}, s16[32,4224]{1,0:T(8,128)(2,1)S(1)}, u32[]{:S(2)}, u32[]{:S(2)}) collective-permute-start(s16[32,4224]{1,0:T(8,128)(2,1)S(1)} %pad_add_fusion.rest_0_), channel_id=1, source_target_pairs={{0,8},{8,0},{16,24},{24,16},{32,40},{40,32},{48,56},{56,48},{64,72... | collective-permute-start | bytes 811016 | tf_op jit(solution)/shard_map/ppermute | solution.py:374
  46.6 12.5 %collective-permute-start.13 = (s16[32,4224]{1,0:T(8,128)(2,1)S(1)}, s16[32,4224]{1,0:T(8,128)(2,1)S(1)}, u32[]{:S(2)}, u32[]{:S(2)}) collective-permute-start(s16[32,4224]{1,0:T(8,128)(2,1)S(1)} %pad_add_fusion.rest_0_), channel_id=1, source_target_pairs={{0,48},{8,56},{16,32},{24,40},{32,16},{40,24},{48,0},{56,8},{64,11... | collective-permute-start | bytes 811016 | tf_op jit(solution)/shard_map/ppermute | solution.py:374
  48.5 39.8 %copy-start = (bf16[256,4096]{1,0:T(8,128)(2,1)S(1)}, bf16[256,4096]{1,0:T(8,128)(2,1)}, u32[]{:S(2)}) copy-start(bf16[256,4096]{1,0:T(8,128)(2,1)} %weights_ref.1) | copy-start | bytes 6291460
  48.5 16.9 %collective-permute-start.12 = (s16[32,4224]{1,0:T(8,128)(2,1)S(1)}, s16[32,4224]{1,0:T(8,128)(2,1)S(1)}, u32[]{:S(2)}, u32[]{:S(2)}) collective-permute-start(s16[32,4224]{1,0:T(8,128)(2,1)S(1)} %pad_add_fusion.rest_0_), channel_id=1, source_target_pairs={{0,16},{8,24},{16,0},{24,8},{32,48},{40,56},{48,32},{56,40},{64,80... | collective-permute-start | bytes 811016 | tf_op jit(solution)/shard_map/ppermute | solution.py:374
  49.0 10.1 %collective-permute-start.6 = (f32[128,512]{1,0:T(8,128)S(1)}, f32[128,512]{1,0:T(8,128)S(1)}, u32[]{:S(2)}, u32[]{:S(2)}) collective-permute-start(f32[128,512]{1,0:T(8,128)S(1)} %pad_maximum_fusion.1), channel_id=1, source_target_pairs={{0,48},{8,56},{16,32},{24,40},{32,16},{40,24},{48,0},{56,8},{64,11... | collective-permute-start | bytes 786440 | tf_op jit(solution)/shard_map/ppermute | solution.py:374
  49.7 15.9 %collective-permute-start.24 = (s16[32,4224]{1,0:T(8,128)(2,1)S(1)}, s16[32,4224]{1,0:T(8,128)(2,1)S(1)}, u32[]{:S(2)}, u32[]{:S(2)}) collective-permute-start(s16[32,4224]{1,0:T(8,128)(2,1)S(1)} %pad_add_fusion.1.rest_4_), channel_id=1, source_target_pairs={{0,8},{8,0},{16,24},{24,16},{32,40},{40,32},{48,56},{56,48},{64,72... | collective-permute-start | bytes 811016 | tf_op jit(solution)/shard_map/ppermute | solution.py:374
  53.4 14.2 %collective-permute-start.17 = (s16[32,4224]{1,0:T(8,128)(2,1)S(1)}, s16[32,4224]{1,0:T(8,128)(2,1)S(1)}, u32[]{:S(2)}, u32[]{:S(2)}) collective-permute-start(s16[32,4224]{1,0:T(8,128)(2,1)S(1)} %pad_add_fusion.1.rest_4_), channel_id=1, source_target_pairs={{0,48},{8,56},{16,32},{24,40},{32,16},{40,24},{48,0},{56,8},{64,11... | collective-permute-start | bytes 811016 | tf_op jit(solution)/shard_map/ppermute | solution.py:374
  59.1 9.6 %collective-permute-start.18 = (s16[32,4224]{1,0:T(8,128)(2,1)S(1)}, s16[32,4224]{1,0:T(8,128)(2,1)S(1)}, u32[]{:S(2)}, u32[]{:S(2)}) collective-permute-start(s16[32,4224]{1,0:T(8,128)(2,1)S(1)} %pad_add_fusion.1.rest_4_), channel_id=1, source_target_pairs={{0,16},{8,24},{16,0},{24,8},{32,48},{40,56},{48,32},{56,40},{64,80... | collective-permute-start | bytes 811016 | tf_op jit(solution)/shard_map/ppermute | solution.py:374
  59.1 21.5 %collective-permute-start.7 = (f32[256,512]{1,0:T(8,128)S(1)}, f32[256,512]{1,0:T(8,128)S(1)}, u32[]{:S(2)}, u32[]{:S(2)}) collective-permute-start(f32[256,512]{1,0:T(8,128)S(1)} %pad_maximum_fusion.own_ref), channel_id=1, source_target_pairs={{0,8},{8,0},{16,24},{24,16},{32,40},{40,32},{48,56},{56,48},{64,72... | collective-permute-start | bytes 1572872 | tf_op jit(solution)/shard_map/ppermute | solution.py:374
  65.5 14.6 %collective-permute-start.22 = (s16[32,4224]{1,0:T(8,128)(2,1)S(1)}, s16[32,4224]{1,0:T(8,128)(2,1)S(1)}, u32[]{:S(2)}, u32[]{:S(2)}) collective-permute-start(s16[32,4224]{1,0:T(8,128)(2,1)S(1)} %collective-permute-done.13.rest_2_), channel_id=1, source_target_pairs={{0,8},{8,0},{16,24},{24,16},{32,40},{40,32},{48,56},{56,48},{64,72... | collective-permute-start | bytes 811016 | tf_op jit(solution)/shard_map/ppermute | solution.py:374
  65.6 14.5 %collective-permute-start.14 = (s16[32,4224]{1,0:T(8,128)(2,1)S(1)}, s16[32,4224]{1,0:T(8,128)(2,1)S(1)}, u32[]{:S(2)}, u32[]{:S(2)}) collective-permute-start(s16[32,4224]{1,0:T(8,128)(2,1)S(1)} %collective-permute-done.12.rest_1_), channel_id=1, source_target_pairs={{0,48},{8,56},{16,32},{24,40},{32,16},{40,24},{48,0},{56,8},{64,11... | collective-permute-start | bytes 811016 | tf_op jit(solution)/shard_map/ppermute | solution.py:374
  67.6 13.0 %collective-permute-start.19 = (s16[32,4224]{1,0:T(8,128)(2,1)S(1)}, s16[32,4224]{1,0:T(8,128)(2,1)S(1)}, u32[]{:S(2)}, u32[]{:S(2)}) collective-permute-start(s16[32,4224]{1,0:T(8,128)(2,1)S(1)} %collective-permute-done.17.rest_5_), channel_id=1, source_target_pairs={{0,16},{8,24},{16,0},{24,8},{32,48},{40,56},{48,32},{56,40},{64,80... | collective-permute-start | bytes 811016 | tf_op jit(solution)/shard_map/ppermute | solution.py:374
  68.7 6.6 %collective-permute-start.10 = (bf16[1024,128]{1,0:T(8,128)(2,1)S(1)}, bf16[1024,128]{1,0:T(8,128)(2,1)S(1)}, u32[]{:S(2)}, u32[]{:S(2)}) collective-permute-start(bf16[1024,128]{1,0:T(8,128)(2,1)S(1)} %pad_maximum_fusion.2.near_ref), channel_id=1, source_target_pairs={{0,3},{1,2},{2,1},{3,0},{4,7},{5,6},{6,5},{7,4},{8,11},{9,10},{10,... | collective-permute-start | bytes 786440 | tf_op jit(solution)/shard_map/ppermute | solution.py:374
  75.3 13.0 %collective-permute-start.21 = (s16[32,4224]{1,0:T(8,128)(2,1)S(1)}, s16[32,4224]{1,0:T(8,128)(2,1)S(1)}, u32[]{:S(2)}, u32[]{:S(2)}) collective-permute-start(s16[32,4224]{1,0:T(8,128)(2,1)S(1)} %collective-permute-done.12.rest_1_), channel_id=1, source_target_pairs={{0,8},{8,0},{16,24},{24,16},{32,40},{40,32},{48,56},{56,48},{64,72... | collective-permute-start | bytes 811016 | tf_op jit(solution)/shard_map/ppermute | solution.py:374
  80.1 8.2 %collective-permute-start.25 = (s16[32,4224]{1,0:T(8,128)(2,1)S(1)}, s16[32,4224]{1,0:T(8,128)(2,1)S(1)}, u32[]{:S(2)}, u32[]{:S(2)}) collective-permute-start(s16[32,4224]{1,0:T(8,128)(2,1)S(1)} %collective-permute-done.17.rest_5_), channel_id=1, source_target_pairs={{0,8},{8,0},{16,24},{24,16},{32,40},{40,32},{48,56},{56,48},{64,72... | collective-permute-start | bytes 811016 | tf_op jit(solution)/shard_map/ppermute | solution.py:374
  80.1 8.2 %collective-permute-start.26 = (s16[32,4224]{1,0:T(8,128)(2,1)S(1)}, s16[32,4224]{1,0:T(8,128)(2,1)S(1)}, u32[]{:S(2)}, u32[]{:S(2)}) collective-permute-start(s16[32,4224]{1,0:T(8,128)(2,1)S(1)} %collective-permute-done.18.rest_6_), channel_id=1, source_target_pairs={{0,8},{8,0},{16,24},{24,16},{32,40},{40,32},{48,56},{56,48},{64,72... | collective-permute-start | bytes 811016 | tf_op jit(solution)/shard_map/ppermute | solution.py:374
  80.6 7.7 %collective-permute-start.23 = (s16[32,4224]{1,0:T(8,128)(2,1)S(1)}, s16[32,4224]{1,0:T(8,128)(2,1)S(1)}, u32[]{:S(2)}, u32[]{:S(2)}) collective-permute-start(s16[32,4224]{1,0:T(8,128)(2,1)S(1)} %collective-permute-done.14.rest_3_), channel_id=1, source_target_pairs={{0,8},{8,0},{16,24},{24,16},{32,40},{40,32},{48,56},{56,48},{64,72... | collective-permute-start | bytes 811016 | tf_op jit(solution)/shard_map/ppermute | solution.py:374
  80.7 7.7 %collective-permute-start.27 = (s16[32,4224]{1,0:T(8,128)(2,1)S(1)}, s16[32,4224]{1,0:T(8,128)(2,1)S(1)}, u32[]{:S(2)}, u32[]{:S(2)}) collective-permute-start(s16[32,4224]{1,0:T(8,128)(2,1)S(1)} %collective-permute-done.19.rest_7_), channel_id=1, source_target_pairs={{0,8},{8,0},{16,24},{24,16},{32,40},{40,32},{48,56},{56,48},{64,72... | collective-permute-start | bytes 811016 | tf_op jit(solution)/shard_map/ppermute | solution.py:374
where the time goes:
time: 95.3 us; the launch traced here: 95.2 us
  starting transfers between devices  54.6 us (57%)
  waiting for transfers between devices  20.2 us (21%)
  Pallas kernels  17.9 us (19%)
  local copies, waits for them, and re-layouts  1.32 us (1%)
  other arithmetic  1.05 us (1%)
    ppermute x28, starting transfers between devices, swap(): return lax.ppermute(value, axis, [(i, i ^ relative) for i in range(size)])  54.6 us
    ppermute x28, waiting for transfers between devices, swap(): return lax.ppermute(value, axis, [(i, i ^ relative) for i in range(size)])  20.2 us
    pallas_call x1, Pallas kernels, update(): pl.pallas_call(update_kernel, out_shape=jax.ShapeDtypeStruct((rows, width...  6.84 us
    pallas_call x1, Pallas kernels, solve(): pl.pallas_call(solve_kernel, out_shape=(jax.ShapeDtypeStruct((rows, order...  6.47 us
    pallas_call x1, Pallas kernels, prepare(): pl.pallas_call(prepare_kernel, out_shape=(jax.ShapeDtypeStruct((height, w...  3.32 us
  transfers between devices with their start and end apart: 28, of which 7 were waited for; matrix products, arithmetic and copies ran while one was open for 1% of the time, Pallas kernels for 8%

commit v1 on v0

--- a/solution.py
+++ b/solution.py
@@ -12,8 +12,10 @@
 MIB = 1 << 20
 TOLERANCE = 3e-5
 DOUBLINGS = 6
+RESIDUAL = 1e-5
 CODE_TOP = 32767.0
 PARTS = 4
+TILE = 512
 CORE, Y_ONE, Y_THREE, Z_ONE, Z_TWO, Z_THREE = 1, 2, 6, 8, 16, 24
 X_ONE, X_THREE, Z_HALF = 1, 3, 4
 OWNER_ORDER = (0, 4, 1, 5, 3, 7, 2, 6)
@@ -39,12 +41,6 @@
 
 def dot(a, b):
     return jnp.dot(a, b, preferred_element_type=f32)
-
-
-def product(a, b):
-    a_high, a_low = halves(a)
-    b_high, b_low = halves(b)
-    return dot(a_high, b_high) + (dot(a_high, b_low) + dot(a_low, b_high))
 
 
 def code_scale(exponent):
@@ -232,7 +228,9 @@
     )(near, far, places)
 
 
-def solve_kernel(own_ref, sibling_ref, columns_ref, high_ref, low_ref, entries_ref, stacked, inverse):
+def solve_kernel(
+    own_ref, sibling_ref, columns_ref, high_ref, low_ref, entries_ref, value, wanted, powers, rest_low, inverse
+):
     order = entries_ref.shape[0]
     rows = columns_ref.shape[0]
     me = lax.axis_index("row")
@@ -250,12 +248,18 @@
     scale_col = lax.rsqrt(jnp.sum(diagonal, axis=1, keepdims=True))
     unit = entries * scale_col * scale_row
     rest = jnp.where(row == col, 1.0 - unit, -unit)
-    stacked[0:rows, :] = columns_ref[...].astype(f32) * scale_row
-    stacked[rows:, :] = rest
-
-    def bound():
-        power = stacked[rows:, :]
-        return jnp.sum(power * power)
+    rest_high = rest.astype(bf16)
+    powers[0:order, :] = rest_high
+    rest_low[...] = (rest - rest_high.astype(f32)).astype(bf16)
+    scaled = columns_ref[...].astype(f32) * scale_row
+    wanted[...] = scaled
+    value[...] = scaled
+
+    def power(index):
+        return powers[pl.ds(pl.multiple_of(index * order, order), order), :]
+
+    def apply(index):
+        value[...] += dot(value[...].astype(bf16), power(index))
 
     def going(state):
         count, left = state
@@ -263,14 +267,21 @@
 
     def double(state):
         count, _ = state
-        power = stacked[rows:, :]
-        result = product(stacked[...], power)
-        stacked[0:rows, :] += result[0:rows, :]
-        stacked[rows:, :] = result[rows:, :]
-        return count + 1, bound()
-
-    _, left = lax.while_loop(going, double, (jnp.int32(0), bound()))
-    settled = left < TOLERANCE
+        this = power(count)
+        apply(count)
+        squared = dot(this, this)
+        powers[pl.ds(pl.multiple_of((count + 1) * order, order), order), :] = squared.astype(bf16)
+        return count + 1, jnp.sum(squared * squared)
+
+    count, _ = lax.while_loop(going, double, (jnp.int32(0), jnp.sum(rest * rest)))
+    apply(count)
+    first = value[...]
+    first_high, first_low = halves(first)
+    through = dot(first_high, power(0)) + (dot(first_high, rest_low[...]) + dot(first_low, power(0)))
+    asked = wanted[...]
+    residual = (asked - first) + through
+    settled = jnp.sum(residual * residual) <= RESIDUAL * jnp.sum(asked * asked)
+    value[...] = residual
 
     def finish(solved):
         index = lax.broadcasted_iota(jnp.int32, (1, order), 1)
@@ -284,8 +295,14 @@
 
     @pl.when(settled)
     def _():
-        solved = stacked[0:rows, :]
-        finish(solved + product(solved, stacked[rows:, :]))
+        inverse[0:rows, :] = first
+
+        def correct(index, carry):
+            apply(index)
+            return carry
+
+        lax.fori_loop(0, count + 1, correct, 0)
+        finish(inverse[0:rows, :] + value[...])
 
     @pl.when(jnp.logical_not(settled))
     def _():
@@ -305,13 +322,13 @@
 
         lax.fori_loop(0, order, pivot, 0)
         whole = entries_ref[...] * scale_col * scale_row
-        wanted = columns_ref[...].astype(f32) * scale_row
+        asked = wanted[...]
 
         def exact(a, b):
             return jnp.dot(a, b, precision=lax.Precision.HIGHEST, preferred_element_type=f32)
 
-        solved = exact(wanted, inverse[...])
-        solved = solved + exact(wanted - exact(solved, whole), inverse[...])
+        solved = exact(asked, inverse[...])
+        solved = solved + exact(asked - exact(solved, whole), inverse[...])
         finish(solved)
 
 
@@ -324,7 +341,10 @@
         out_specs=(vmem_spec(), vmem_spec()),
         scratch_shapes=[
             VMEM((order, order), f32),
-            VMEM((rows + order, order), f32),
+            VMEM((rows, order), f32),
+            VMEM((rows, order), f32),
+            VMEM(((DOUBLINGS + 1) * order, order), bf16),
+            VMEM((order, order), bf16),
             VMEM((order, order), f32),
         ],
         name="solve",
@@ -333,37 +353,58 @@
 
 
 def update_kernel(weights_ref, high_ref, low_ref, *rest):
-    panels, out_ref = rest[:-1], rest[-1]
-    tile = weights_ref.shape[1]
+    panels, out_ref = rest[:-7], rest[-7]
+    coefs_high, coefs_low = rest[-6:-4]
+    even, odd = rest[-4:-2], rest[-2:]
+    step = pl.program_id(0)
+    tile = weights_ref.shape[1] // 2
     width = panels[0].shape[1] - 128
-    start = pl.multiple_of(pl.program_id(0) * tile, tile)
-    pieces = []
-    for ref in panels:
-        scale = code_scale(ref[:, width:].astype(jnp.int32))[:, 0:1]
-        code = ref[:, pl.ds(start, tile)].astype(jnp.int32).astype(f32)
-        pieces.append(halves(code * jnp.abs(code) * scale))
-    panel_high = jnp.concatenate([p[0] for p in pieces], axis=0)
-    panel_low = jnp.concatenate([p[1] for p in pieces], axis=0)
-    high = high_ref[...]
-    change = dot(high, panel_high) + (dot(high, panel_low) + dot(low_ref[...], panel_high))
-    out_ref[...] = (weights_ref[...].astype(f32) - change).astype(bf16)
+
+    def decode(index, target):
+        start = pl.multiple_of(index * tile, tile)
+        at = 0
+        for ref in panels:
+            code = ref[:, pl.ds(start, tile)].astype(jnp.int32).astype(f32)
+            high, low = halves(code * jnp.abs(code))
+            target[0][at : at + ref.shape[0], :] = high
+            target[1][at : at + ref.shape[0], :] = low
+            at += ref.shape[0]
+
+    def change(source):
+        high = coefs_high[...]
+        panel_high = source[0][...]
+        return dot(high, panel_high) + (dot(high, source[1][...]) + dot(coefs_low[...], panel_high))
+
+    @pl.when(step == 0)
+    def _():
+        exponents = jnp.concatenate([ref[:, width:].astype(jnp.int32).astype(f32) for ref in panels], axis=0)
+        scale = jnp.exp2(jnp.transpose(exponents)[0:1, :] * 0.125)
+        high, low = halves((high_ref[...].astype(f32) + low_ref[...].astype(f32)) * scale)
+        coefs_high[...] = high
+        coefs_low[...] = low
+        decode(0, even)
+
+    decode(2 * step + 1, odd)
+    out_ref[:, 0:tile] = (weights_ref[:, 0:tile].astype(f32) - change(even)).astype(bf16)
+    decode(jnp.minimum(2 * step + 2, width // tile - 1), even)
+    out_ref[:, tile:] = (weights_ref[:, tile:].astype(f32) - change(odd)).astype(bf16)
 
 
 def update(weights, high, low, panels):
     rows, width = weights.shape
     order = high.shape[1]
-    tile = 512
     return pl.pallas_call(
         update_kernel,
         out_shape=jax.ShapeDtypeStruct((rows, width), bf16),
-        grid=(width // tile,),
+        grid=(width // (2 * TILE),),
         in_specs=[
-            pl.BlockSpec((rows, tile), lambda i: (0, i)),
+            pl.BlockSpec((rows, 2 * TILE), lambda i: (0, i)),
             pl.BlockSpec((rows, order), lambda i: (0, 0)),
             pl.BlockSpec((rows, order), lambda i: (0, 0)),
         ]
         + [vmem_spec()] * len(panels),
-        out_specs=pl.BlockSpec((rows, tile), lambda i: (0, i)),
+        out_specs=pl.BlockSpec((rows, 2 * TILE), lambda i: (0, i)),
+        scratch_shapes=[VMEM((rows, order), bf16)] * 2 + [VMEM((order, TILE), bf16)] * 4,
         name="update",
         compiler_params=pltpu.CompilerParams(vmem_limit_bytes=24 * MIB),
     )(weights, high, low, *panels)

time: 95.3 us -> 93.8 us (0.984)
  Pallas kernels: 17.9 us -> 16.4 us
  transfers between devices with their start and end apart: 28 -> 28, of which waited for: 7 -> 7; matrix products, arithmetic and copies ran while one was open for 1% -> 1% of each run, Pallas kernels for 8% -> 7%
where the time goes in v1:
time: 93.8 us; the launch traced here: 93.7 us
  starting transfers between devices  54.6 us (58%)
  waiting for transfers between devices  20.2 us (22%)
  Pallas kernels  16.4 us (17%)
  local copies, waits for them, and re-layouts  1.32 us (1%)
  other arithmetic  1.05 us (1%)
    ppermute x28, starting transfers between devices, swap(): return lax.ppermute(value, axis, [(i, i ^ relative) for i in range(size)])  54.6 us
    ppermute x28, waiting for transfers between devices, swap(): return lax.ppermute(value, axis, [(i, i ^ relative) for i in range(size)])  20.2 us
    pallas_call x1, Pallas kernels, update(): pl.pallas_call(update_kernel, out_shape=jax.ShapeDtypeStruct((rows, width...  5.91 us
    pallas_call x1, Pallas kernels, solve(): pl.pallas_call(solve_kernel, out_shape=(jax.ShapeDtypeStruct((rows, order...  5.9 us
    pallas_call x1, Pallas kernels, prepare(): pl.pallas_call(prepare_kernel, out_shape=(jax.ShapeDtypeStruct((height, w...  3.32 us
  transfers between devices with their start and end apart: 28, of which 7 were waited for; matrix products, arithmetic and copies ran while one was open for 1% of the time, Pallas kernels for 7%

profile of v1, /device:TPU:1, one launch (start us, length us, event | category | flops | bytes accessed | tf_op | source)
XLA Modules:
  0.0 93.7 jit_solution(12101401221382871004)
XLA Ops:
  0.0 0.7 copy-done.1
  0.7 0.7 copy-done.2
  1.3 3.3 %prepare.1 = (s16[16,4224]{1,0:T(8,128)(2,1)}, bf16[64,128]{1,0:T(8,128)(2,1)S(1)}, bf16[256,128]{1,0:T(8,128)(2,1)S(1)}) custom-call(f32[8,4096]{1,0:T(8,128)} %first_hbm.1, f32[8,4096]{1,0:T(8,128)} %second_hbm.1, s32[1,64]{1,0:T(1,128)S(1)} %bitcast.2, s32[1,64]{1,0:T(1,128)S(1)} %bitcast.3, bf16[256,4096]{1,0:T(8,128)(2,1)} %weights_ref.1), custom_call_target="tpu_custom_call" | custom-call | tf_op jit(solution)/shard_map/prepare/pallas_call | solution.py:120
  4.6 7.8 %collective-permute-start = (bf16[64,128]{1,0:T(8,128)(2,1)S(1)}, bf16[64,128]{1,0:T(8,128)(2,1)S(1)}, u32[]{:S(2)}, u32[]{:S(2)}) collective-permute-start(bf16[64,128]{1,0:T(8,128)(2,1)S(1)} %get-tuple-element.12), channel_id=1, source_target_pairs={{0,4},{1,5},{2,6},{3,7},{4,0},{5,1},{6,2},{7,3},{8,12},{9,13},{10,... | collective-permute-start | bytes 49160 | tf_op jit(solution)/shard_map/ppermute | solution.py:415
  12.5 1.1 %collective-permute-done = bf16[64,128]{1,0:T(8,128)(2,1)S(1)} collective-permute-done((bf16[64,128]{1,0:T(8,128)(2,1)S(1)}, bf16[64,128]{1,0:T(8,128)(2,1)S(1)}, u32[]{:S(2)}, u32[]{:S(2)}) %collective-permute-start) | collective-permute-done | bytes 16416 | tf_op jit(solution)/shard_map/ppermute | solution.py:415
  13.6 1.2 %collective-permute-start.1 = (bf16[128,128]{1,0:T(8,128)(2,1)S(1)}, bf16[128,128]{1,0:T(8,128)(2,1)S(1)}, u32[]{:S(2)}, u32[]{:S(2)}) collective-permute-start(bf16[128,128]{1,0:T(8,128)(2,1)S(1)} %pad_maximum_fusion.7), channel_id=1, source_target_pairs={{0,1},{1,0},{2,3},{3,2},{4,5},{5,4},{6,7},{7,6},{8,9},{9,8},{10,11... | collective-permute-start | bytes 98312 | tf_op jit(solution)/shard_map/ppermute | solution.py:415
  14.8 1.6 %collective-permute-done.1 = bf16[128,128]{1,0:T(8,128)(2,1)S(1)} collective-permute-done((bf16[128,128]{1,0:T(8,128)(2,1)S(1)}, bf16[128,128]{1,0:T(8,128)(2,1)S(1)}, u32[]{:S(2)}, u32[]{:S(2)}) %collective-permute-start.1) | collective-permute-done | bytes 32800 | tf_op jit(solution)/shard_map/ppermute | solution.py:415
  16.4 2.5 %collective-permute-start.2 = (bf16[256,128]{1,0:T(8,128)(2,1)S(1)}, bf16[256,128]{1,0:T(8,128)(2,1)S(1)}, u32[]{:S(2)}, u32[]{:S(2)}) collective-permute-start(bf16[256,128]{1,0:T(8,128)(2,1)S(1)} %pad_maximum_fusion.5.near_ref), channel_id=1, source_target_pairs={{0,3},{1,2},{2,1},{3,0},{4,7},{5,6},{6,5},{7,4},{8,11},{9,10},{10,... | collective-permute-start | bytes 196616 | tf_op jit(solution)/shard_map/ppermute | solution.py:415
  18.8 1.9 %collective-permute-done.2.far_ref = bf16[256,128]{1,0:T(8,128)(2,1)S(1)} collective-permute-done((bf16[256,128]{1,0:T(8,128)(2,1)S(1)}, bf16[256,128]{1,0:T(8,128)(2,1)S(1)}, u32[]{:S(2)}, u32[]{:S(2)}) %collective-permute-start.2) | collective-permute-done | bytes 65568 | tf_op jit(solution)/shard_map/ppermute | solution.py:415
  21.3 0.8 collective-permute-start.3
  22.0 2.1 %collective-permute-start.16 = (s16[16,4224]{1,0:T(8,128)(2,1)}, s16[16,4224]{1,0:T(8,128)(2,1)S(1)}, u32[]{:S(2)}, u32[]{:S(2)}) collective-permute-start(s16[16,4224]{1,0:T(8,128)(2,1)} %get-tuple-element.18), channel_id=1, source_target_pairs={{0,192},{8,200},{16,208},{24,216},{32,224},{40,232},{48,240},{56,2... | collective-permute-start | bytes 405512 | tf_op jit(solution)/shard_map/ppermute | solution.py:415
  24.4 1.2 %collective-permute-start.11 = (s16[16,4224]{1,0:T(8,128)(2,1)}, s16[16,4224]{1,0:T(8,128)(2,1)S(1)}, u32[]{:S(2)}, u32[]{:S(2)}) collective-permute-start(s16[16,4224]{1,0:T(8,128)(2,1)} %get-tuple-element.18), channel_id=1, source_target_pairs={{0,64},{8,72},{16,80},{24,88},{32,96},{40,104},{48,112},{56,120},{... | collective-permute-start | bytes 405512 | tf_op jit(solution)/shard_map/ppermute | solution.py:415
  25.6 5.4 %collective-permute-start.8 = (bf16[256,128]{1,0:T(8,128)(2,1)S(1)}, bf16[256,128]{1,0:T(8,128)(2,1)S(1)}, u32[]{:S(2)}, u32[]{:S(2)}) collective-permute-start(bf16[256,128]{1,0:T(8,128)(2,1)S(1)} %get-tuple-element.14), channel_id=1, source_target_pairs={{0,4},{1,5},{2,6},{3,7},{4,0},{5,1},{6,2},{7,3},{8,12},{9,13},{10,... | collective-permute-start | bytes 196616 | tf_op jit(solution)/shard_map/ppermute | solution.py:415
  31.5 4.9 %collective-permute-done.8 = bf16[256,128]{1,0:T(8,128)(2,1)S(1)} collective-permute-done((bf16[256,128]{1,0:T(8,128)(2,1)S(1)}, bf16[256,128]{1,0:T(8,128)(2,1)S(1)}, u32[]{:S(2)}, u32[]{:S(2)}) %collective-permute-start.8) | collective-permute-done | bytes 65568 | tf_op jit(solution)/shard_map/ppermute | solution.py:415
  36.5 2.7 %collective-permute-done.4 = f32[32,512]{1,0:T(8,128)S(1)} collective-permute-done((f32[32,512]{1,0:T(8,128)S(1)}, f32[32,512]{1,0:T(8,128)S(1)}, u32[]{:S(2)}, u32[]{:S(2)}) %collective-permute-start.4) | collective-permute-done | bytes 65568 | tf_op jit(solution)/shard_map/ppermute | solution.py:415
  39.2 1.4 %collective-permute-start.5 = (f32[64,512]{1,0:T(8,128)S(1)}, f32[64,512]{1,0:T(8,128)S(1)}, u32[]{:S(2)}, u32[]{:S(2)}) collective-permute-start(f32[64,512]{1,0:T(8,128)S(1)} %pad_maximum_fusion.3), channel_id=1, source_target_pairs={{0,16},{8,24},{16,0},{24,8},{32,48},{40,56},{48,32},{56,40},{64,80... | collective-permute-start | bytes 393224 | tf_op jit(solution)/shard_map/ppermute | solution.py:415
  40.6 0.9 pad_add_fusion.rest_0_
  41.5 5.1 %collective-permute-start.20 = (s16[32,4224]{1,0:T(8,128)(2,1)S(1)}, s16[32,4224]{1,0:T(8,128)(2,1)S(1)}, u32[]{:S(2)}, u32[]{:S(2)}) collective-permute-start(s16[32,4224]{1,0:T(8,128)(2,1)S(1)} %pad_add_fusion.rest_0_), channel_id=1, source_target_pairs={{0,8},{8,0},{16,24},{24,16},{32,40},{40,32},{48,56},{56,48},{64,72... | collective-permute-start | bytes 811016 | tf_op jit(solution)/shard_map/ppermute | solution.py:415
  46.6 1.9 %collective-permute-start.13 = (s16[32,4224]{1,0:T(8,128)(2,1)S(1)}, s16[32,4224]{1,0:T(8,128)(2,1)S(1)}, u32[]{:S(2)}, u32[]{:S(2)}) collective-permute-start(s16[32,4224]{1,0:T(8,128)(2,1)S(1)} %pad_add_fusion.rest_0_), channel_id=1, source_target_pairs={{0,48},{8,56},{16,32},{24,40},{32,16},{40,24},{48,0},{56,8},{64,11... | collective-permute-start | bytes 811016 | tf_op jit(solution)/shard_map/ppermute | solution.py:415
  49.0 0.6 collective-permute-start.6
  49.7 3.8 %collective-permute-start.24 = (s16[32,4224]{1,0:T(8,128)(2,1)S(1)}, s16[32,4224]{1,0:T(8,128)(2,1)S(1)}, u32[]{:S(2)}, u32[]{:S(2)}) collective-permute-start(s16[32,4224]{1,0:T(8,128)(2,1)S(1)} %pad_add_fusion.1.rest_4_), channel_id=1, source_target_pairs={{0,8},{8,0},{16,24},{24,16},{32,40},{40,32},{48,56},{56,48},{64,72... | collective-permute-start | bytes 811016 | tf_op jit(solution)/shard_map/ppermute | solution.py:415
  53.4 1.9 %collective-permute-start.17 = (s16[32,4224]{1,0:T(8,128)(2,1)S(1)}, s16[32,4224]{1,0:T(8,128)(2,1)S(1)}, u32[]{:S(2)}, u32[]{:S(2)}) collective-permute-start(s16[32,4224]{1,0:T(8,128)(2,1)S(1)} %pad_add_fusion.1.rest_4_), channel_id=1, source_target_pairs={{0,48},{8,56},{16,32},{24,40},{32,16},{40,24},{48,0},{56,8},{64,11... | collective-permute-start | bytes 811016 | tf_op jit(solution)/shard_map/ppermute | solution.py:415
  55.3 3.8 %collective-permute-done.6 = f32[128,512]{1,0:T(8,128)S(1)} collective-permute-done((f32[128,512]{1,0:T(8,128)S(1)}, f32[128,512]{1,0:T(8,128)S(1)}, u32[]{:S(2)}, u32[]{:S(2)}) %collective-permute-start.6) | collective-permute-done | bytes 262176 | tf_op jit(solution)/shard_map/ppermute | solution.py:415
  59.1 6.3 %collective-permute-start.7 = (f32[256,512]{1,0:T(8,128)S(1)}, f32[256,512]{1,0:T(8,128)S(1)}, u32[]{:S(2)}, u32[]{:S(2)}) collective-permute-start(f32[256,512]{1,0:T(8,128)S(1)} %pad_maximum_fusion.own_ref), channel_id=1, source_target_pairs={{0,8},{8,0},{16,24},{24,16},{32,40},{40,32},{48,56},{56,48},{64,72... | collective-permute-start | bytes 1572872 | tf_op jit(solution)/shard_map/ppermute | solution.py:415
  65.6 2.0 %collective-permute-start.14 = (s16[32,4224]{1,0:T(8,128)(2,1)S(1)}, s16[32,4224]{1,0:T(8,128)(2,1)S(1)}, u32[]{:S(2)}, u32[]{:S(2)}) collective-permute-start(s16[32,4224]{1,0:T(8,128)(2,1)S(1)} %collective-permute-done.12.rest_1_), channel_id=1, source_target_pairs={{0,48},{8,56},{16,32},{24,40},{32,16},{40,24},{48,0},{56,8},{64,11... | collective-permute-start | bytes 811016 | tf_op jit(solution)/shard_map/ppermute | solution.py:415
  67.6 1.1 %collective-permute-start.19 = (s16[32,4224]{1,0:T(8,128)(2,1)S(1)}, s16[32,4224]{1,0:T(8,128)(2,1)S(1)}, u32[]{:S(2)}, u32[]{:S(2)}) collective-permute-start(s16[32,4224]{1,0:T(8,128)(2,1)S(1)} %collective-permute-done.17.rest_5_), channel_id=1, source_target_pairs={{0,16},{8,24},{16,0},{24,8},{32,48},{40,56},{48,32},{56,40},{64,80... | collective-permute-start | bytes 811016 | tf_op jit(solution)/shard_map/ppermute | solution.py:415
  68.7 2.3 %collective-permute-start.10 = (bf16[1024,128]{1,0:T(8,128)(2,1)S(1)}, bf16[1024,128]{1,0:T(8,128)(2,1)S(1)}, u32[]{:S(2)}, u32[]{:S(2)}) collective-permute-start(bf16[1024,128]{1,0:T(8,128)(2,1)S(1)} %pad_maximum_fusion.2.near_ref), channel_id=1, source_target_pairs={{0,3},{1,2},{2,1},{3,0},{4,7},{5,6},{6,5},{7,4},{8,11},{9,10},{10,... | collective-permute-start | bytes 786440 | tf_op jit(solution)/shard_map/ppermute | solution.py:415
  71.0 4.3 %collective-permute-done.10.far_ref = bf16[1024,128]{1,0:T(8,128)(2,1)S(1)} collective-permute-done((bf16[1024,128]{1,0:T(8,128)(2,1)S(1)}, bf16[1024,128]{1,0:T(8,128)(2,1)S(1)}, u32[]{:S(2)}, u32[]{:S(2)}) %collective-permute-start.10) | collective-permute-done | bytes 262176 | tf_op jit(solution)/shard_map/ppermute | solution.py:415
  75.3 4.8 %collective-permute-start.21 = (s16[32,4224]{1,0:T(8,128)(2,1)S(1)}, s16[32,4224]{1,0:T(8,128)(2,1)S(1)}, u32[]{:S(2)}, u32[]{:S(2)}) collective-permute-start(s16[32,4224]{1,0:T(8,128)(2,1)S(1)} %collective-permute-done.12.rest_1_), channel_id=1, source_target_pairs={{0,8},{8,0},{16,24},{24,16},{32,40},{40,32},{48,56},{56,48},{64,72... | collective-permute-start | bytes 811016 | tf_op jit(solution)/shard_map/ppermute | solution.py:415
  81.1 0.7 place.1.columns_ref
  81.8 5.9 %solve.1 = (bf16[256,512]{1,0:T(8,128)(2,1)S(1)}, bf16[256,512]{1,0:T(8,128)(2,1)S(1)}) custom-call(f32[256,512]{1,0:T(8,128)S(1)} %pad_maximum_fusion.own_ref, f32[256,512]{1,0:T(8,128)S(1)} %collective-permute-done.7.sibling_ref, bf16[256,512]{1,0:T(8,128)(2,1)S(1)} %place.1.columns_ref), custom_call_target="tpu_custom_call" | custom-call | tf_op jit(solution)/shard_map/solve/pallas_call | solution.py:337
  87.8 5.9 %update.1 = bf16[256,4096]{1,0:T(8,128)(2,1)} custom-call(bf16[256,4096]{1,0:T(8,128)(2,1)S(1)} %copy-done, bf16[256,512]{1,0:T(8,128)(2,1)S(1)} %get-tuple-element.16.high_ref, bf16[256,512]{1,0:T(8,128)(2,1)S(1)} %get-tuple-element.17.low_ref, s16[32,4224]{1,0:T(8,128)(2,1)S(1)} %pad_add_fusion.rest_0_, ...), custom_call_target="tpu_custom_call" | custom-call | tf_op jit(solution)/shard_map/update/pallas_call | solution.py:396
  (45 shorter events, 3.3 us)
Async XLA Ops:
  0.0 0.7 copy-start.1
  0.7 0.7 copy-start.2
  4.6 8.9 %collective-permute-start = (bf16[64,128]{1,0:T(8,128)(2,1)S(1)}, bf16[64,128]{1,0:T(8,128)(2,1)S(1)}, u32[]{:S(2)}, u32[]{:S(2)}) collective-permute-start(bf16[64,128]{1,0:T(8,128)(2,1)S(1)} %get-tuple-element.12), channel_id=1, source_target_pairs={{0,4},{1,5},{2,6},{3,7},{4,0},{5,1},{6,2},{7,3},{8,12},{9,13},{10,... | collective-permute-start | bytes 49160 | tf_op jit(solution)/shard_map/ppermute | solution.py:415
  13.6 2.8 %collective-permute-start.1 = (bf16[128,128]{1,0:T(8,128)(2,1)S(1)}, bf16[128,128]{1,0:T(8,128)(2,1)S(1)}, u32[]{:S(2)}, u32[]{:S(2)}) collective-permute-start(bf16[128,128]{1,0:T(8,128)(2,1)S(1)} %pad_maximum_fusion.7), channel_id=1, source_target_pairs={{0,1},{1,0},{2,3},{3,2},{4,5},{5,4},{6,7},{7,6},{8,9},{9,8},{10,11... | collective-permute-start | bytes 98312 | tf_op jit(solution)/shard_map/ppermute | solution.py:415
  16.4 4.3 %collective-permute-start.2 = (bf16[256,128]{1,0:T(8,128)(2,1)S(1)}, bf16[256,128]{1,0:T(8,128)(2,1)S(1)}, u32[]{:S(2)}, u32[]{:S(2)}) collective-permute-start(bf16[256,128]{1,0:T(8,128)(2,1)S(1)} %pad_maximum_fusion.5.near_ref), channel_id=1, source_target_pairs={{0,3},{1,2},{2,1},{3,0},{4,7},{5,6},{6,5},{7,4},{8,11},{9,10},{10,... | collective-permute-start | bytes 196616 | tf_op jit(solution)/shard_map/ppermute | solution.py:415
  21.3 9.7 %collective-permute-start.3 = (f32[16,512]{1,0:T(8,128)S(1)}, f32[16,512]{1,0:T(8,128)S(1)}, u32[]{:S(2)}, u32[]{:S(2)}) collective-permute-start(f32[16,512]{1,0:T(8,128)S(1)} %get-tuple-element.13), channel_id=1, source_target_pairs={{0,64},{8,72},{16,80},{24,88},{32,96},{40,104},{48,112},{56,120},{... | collective-permute-start | bytes 98312 | tf_op jit(solution)/shard_map/ppermute | solution.py:415
  22.0 26.5 %collective-permute-start.16 = (s16[16,4224]{1,0:T(8,128)(2,1)}, s16[16,4224]{1,0:T(8,128)(2,1)S(1)}, u32[]{:S(2)}, u32[]{:S(2)}) collective-permute-start(s16[16,4224]{1,0:T(8,128)(2,1)} %get-tuple-element.18), channel_id=1, source_target_pairs={{0,192},{8,200},{16,208},{24,216},{32,224},{40,232},{48,240},{56,2... | collective-permute-start | bytes 405512 | tf_op jit(solution)/shard_map/ppermute | solution.py:415
  24.2 24.9 %collective-permute-start.15 = (s16[16,4224]{1,0:T(8,128)(2,1)}, s16[16,4224]{1,0:T(8,128)(2,1)S(1)}, u32[]{:S(2)}, u32[]{:S(2)}) collective-permute-start(s16[16,4224]{1,0:T(8,128)(2,1)} %get-tuple-element.18), channel_id=1, source_target_pairs={{0,128},{8,136},{16,144},{24,152},{32,160},{40,168},{48,176},{56,1... | collective-permute-start | bytes 405512 | tf_op jit(solution)/shard_map/ppermute | solution.py:415
  24.4 16.2 %collective-permute-start.11 = (s16[16,4224]{1,0:T(8,128)(2,1)}, s16[16,4224]{1,0:T(8,128)(2,1)S(1)}, u32[]{:S(2)}, u32[]{:S(2)}) collective-permute-start(s16[16,4224]{1,0:T(8,128)(2,1)} %get-tuple-element.18), channel_id=1, source_target_pairs={{0,64},{8,72},{16,80},{24,88},{32,96},{40,104},{48,112},{56,120},{... | collective-permute-start | bytes 405512 | tf_op jit(solution)/shard_map/ppermute | solution.py:415
  25.6 10.8 %collective-permute-start.8 = (bf16[256,128]{1,0:T(8,128)(2,1)S(1)}, bf16[256,128]{1,0:T(8,128)(2,1)S(1)}, u32[]{:S(2)}, u32[]{:S(2)}) collective-permute-start(bf16[256,128]{1,0:T(8,128)(2,1)S(1)} %get-tuple-element.14), channel_id=1, source_target_pairs={{0,4},{1,5},{2,6},{3,7},{4,0},{5,1},{6,2},{7,3},{8,12},{9,13},{10,... | collective-permute-start | bytes 196616 | tf_op jit(solution)/shard_map/ppermute | solution.py:415
  31.0 8.3 %collective-permute-start.4 = (f32[32,512]{1,0:T(8,128)S(1)}, f32[32,512]{1,0:T(8,128)S(1)}, u32[]{:S(2)}, u32[]{:S(2)}) collective-permute-start(f32[32,512]{1,0:T(8,128)S(1)} %pad_maximum_fusion.6), channel_id=1, source_target_pairs={{0,128},{8,136},{16,144},{24,152},{32,160},{40,168},{48,176},{56,1... | collective-permute-start | bytes 196616 | tf_op jit(solution)/shard_map/ppermute | solution.py:415
  36.4 13.3 %collective-permute-start.9 = (bf16[512,128]{1,0:T(8,128)(2,1)S(1)}, bf16[512,128]{1,0:T(8,128)(2,1)S(1)}, u32[]{:S(2)}, u32[]{:S(2)}) collective-permute-start(bf16[512,128]{1,0:T(8,128)(2,1)S(1)} %pad_maximum_fusion.4), channel_id=1, source_target_pairs={{0,1},{1,0},{2,3},{3,2},{4,5},{5,4},{6,7},{7,6},{8,9},{9,8},{10,11... | collective-permute-start | bytes 393224 | tf_op jit(solution)/shard_map/ppermute | solution.py:415
  39.2 7.4 %collective-permute-start.5 = (f32[64,512]{1,0:T(8,128)S(1)}, f32[64,512]{1,0:T(8,128)S(1)}, u32[]{:S(2)}, u32[]{:S(2)}) collective-permute-start(f32[64,512]{1,0:T(8,128)S(1)} %pad_maximum_fusion.3), channel_id=1, source_target_pairs={{0,16},{8,24},{16,0},{24,8},{32,48},{40,56},{48,32},{56,40},{64,80... | collective-permute-start | bytes 393224 | tf_op jit(solution)/shard_map/ppermute | solution.py:415
  41.5 11.9 %collective-permute-start.20 = (s16[32,4224]{1,0:T(8,128)(2,1)S(1)}, s16[32,4224]{1,0:T(8,128)(2,1)S(1)}, u32[]{:S(2)}, u32[]{:S(2)}) collective-permute-start(s16[32,4224]{1,0:T(8,128)(2,1)S(1)} %pad_add_fusion.rest_0_), channel_id=1, source_target_pairs={{0,8},{8,0},{16,24},{24,16},{32,40},{40,32},{48,56},{56,48},{64,72... | collective-permute-start | bytes 811016 | tf_op jit(solution)/shard_map/ppermute | solution.py:415
  46.6 12.5 %collective-permute-start.13 = (s16[32,4224]{1,0:T(8,128)(2,1)S(1)}, s16[32,4224]{1,0:T(8,128)(2,1)S(1)}, u32[]{:S(2)}, u32[]{:S(2)}) collective-permute-start(s16[32,4224]{1,0:T(8,128)(2,1)S(1)} %pad_add_fusion.rest_0_), channel_id=1, source_target_pairs={{0,48},{8,56},{16,32},{24,40},{32,16},{40,24},{48,0},{56,8},{64,11... | collective-permute-start | bytes 811016 | tf_op jit(solution)/shard_map/ppermute | solution.py:415
  48.5 39.3 %copy-start = (bf16[256,4096]{1,0:T(8,128)(2,1)S(1)}, bf16[256,4096]{1,0:T(8,128)(2,1)}, u32[]{:S(2)}) copy-start(bf16[256,4096]{1,0:T(8,128)(2,1)} %weights_ref.1) | copy-start | bytes 6291460
  48.5 16.9 %collective-permute-start.12 = (s16[32,4224]{1,0:T(8,128)(2,1)S(1)}, s16[32,4224]{1,0:T(8,128)(2,1)S(1)}, u32[]{:S(2)}, u32[]{:S(2)}) collective-permute-start(s16[32,4224]{1,0:T(8,128)(2,1)S(1)} %pad_add_fusion.rest_0_), channel_id=1, source_target_pairs={{0,16},{8,24},{16,0},{24,8},{32,48},{40,56},{48,32},{56,40},{64,80... | collective-permute-start | bytes 811016 | tf_op jit(solution)/shard_map/ppermute | solution.py:415
  49.0 10.1 %collective-permute-start.6 = (f32[128,512]{1,0:T(8,128)S(1)}, f32[128,512]{1,0:T(8,128)S(1)}, u32[]{:S(2)}, u32[]{:S(2)}) collective-permute-start(f32[128,512]{1,0:T(8,128)S(1)} %pad_maximum_fusion.1), channel_id=1, source_target_pairs={{0,48},{8,56},{16,32},{24,40},{32,16},{40,24},{48,0},{56,8},{64,11... | collective-permute-start | bytes 786440 | tf_op jit(solution)/shard_map/ppermute | solution.py:415
  49.7 15.9 %collective-permute-start.24 = (s16[32,4224]{1,0:T(8,128)(2,1)S(1)}, s16[32,4224]{1,0:T(8,128)(2,1)S(1)}, u32[]{:S(2)}, u32[]{:S(2)}) collective-permute-start(s16[32,4224]{1,0:T(8,128)(2,1)S(1)} %pad_add_fusion.1.rest_4_), channel_id=1, source_target_pairs={{0,8},{8,0},{16,24},{24,16},{32,40},{40,32},{48,56},{56,48},{64,72... | collective-permute-start | bytes 811016 | tf_op jit(solution)/shard_map/ppermute | solution.py:415
  53.4 14.2 %collective-permute-start.17 = (s16[32,4224]{1,0:T(8,128)(2,1)S(1)}, s16[32,4224]{1,0:T(8,128)(2,1)S(1)}, u32[]{:S(2)}, u32[]{:S(2)}) collective-permute-start(s16[32,4224]{1,0:T(8,128)(2,1)S(1)} %pad_add_fusion.1.rest_4_), channel_id=1, source_target_pairs={{0,48},{8,56},{16,32},{24,40},{32,16},{40,24},{48,0},{56,8},{64,11... | collective-permute-start | bytes 811016 | tf_op jit(solution)/shard_map/ppermute | solution.py:415
  59.1 9.6 %collective-permute-start.18 = (s16[32,4224]{1,0:T(8,128)(2,1)S(1)}, s16[32,4224]{1,0:T(8,128)(2,1)S(1)}, u32[]{:S(2)}, u32[]{:S(2)}) collective-permute-start(s16[32,4224]{1,0:T(8,128)(2,1)S(1)} %pad_add_fusion.1.rest_4_), channel_id=1, source_target_pairs={{0,16},{8,24},{16,0},{24,8},{32,48},{40,56},{48,32},{56,40},{64,80... | collective-permute-start | bytes 811016 | tf_op jit(solution)/shard_map/ppermute | solution.py:415
  59.1 21.5 %collective-permute-start.7 = (f32[256,512]{1,0:T(8,128)S(1)}, f32[256,512]{1,0:T(8,128)S(1)}, u32[]{:S(2)}, u32[]{:S(2)}) collective-permute-start(f32[256,512]{1,0:T(8,128)S(1)} %pad_maximum_fusion.own_ref), channel_id=1, source_target_pairs={{0,8},{8,0},{16,24},{24,16},{32,40},{40,32},{48,56},{56,48},{64,72... | collective-permute-start | bytes 1572872 | tf_op jit(solution)/shard_map/ppermute | solution.py:415
  65.5 14.6 %collective-permute-start.22 = (s16[32,4224]{1,0:T(8,128)(2,1)S(1)}, s16[32,4224]{1,0:T(8,128)(2,1)S(1)}, u32[]{:S(2)}, u32[]{:S(2)}) collective-permute-start(s16[32,4224]{1,0:T(8,128)(2,1)S(1)} %collective-permute-done.13.rest_2_), channel_id=1, source_target_pairs={{0,8},{8,0},{16,24},{24,16},{32,40},{40,32},{48,56},{56,48},{64,72... | collective-permute-start | bytes 811016 | tf_op jit(solution)/shard_map/ppermute | solution.py:415
  65.6 14.5 %collective-permute-start.14 = (s16[32,4224]{1,0:T(8,128)(2,1)S(1)}, s16[32,4224]{1,0:T(8,128)(2,1)S(1)}, u32[]{:S(2)}, u32[]{:S(2)}) collective-permute-start(s16[32,4224]{1,0:T(8,128)(2,1)S(1)} %collective-permute-done.12.rest_1_), channel_id=1, source_target_pairs={{0,48},{8,56},{16,32},{24,40},{32,16},{40,24},{48,0},{56,8},{64,11... | collective-permute-start | bytes 811016 | tf_op jit(solution)/shard_map/ppermute | solution.py:415
  67.6 13.0 %collective-permute-start.19 = (s16[32,4224]{1,0:T(8,128)(2,1)S(1)}, s16[32,4224]{1,0:T(8,128)(2,1)S(1)}, u32[]{:S(2)}, u32[]{:S(2)}) collective-permute-start(s16[32,4224]{1,0:T(8,128)(2,1)S(1)} %collective-permute-done.17.rest_5_), channel_id=1, source_target_pairs={{0,16},{8,24},{16,0},{24,8},{32,48},{40,56},{48,32},{56,40},{64,80... | collective-permute-start | bytes 811016 | tf_op jit(solution)/shard_map/ppermute | solution.py:415
  68.7 6.6 %collective-permute-start.10 = (bf16[1024,128]{1,0:T(8,128)(2,1)S(1)}, bf16[1024,128]{1,0:T(8,128)(2,1)S(1)}, u32[]{:S(2)}, u32[]{:S(2)}) collective-permute-start(bf16[1024,128]{1,0:T(8,128)(2,1)S(1)} %pad_maximum_fusion.2.near_ref), channel_id=1, source_target_pairs={{0,3},{1,2},{2,1},{3,0},{4,7},{5,6},{6,5},{7,4},{8,11},{9,10},{10,... | collective-permute-start | bytes 786440 | tf_op jit(solution)/shard_map/ppermute | solution.py:415
  75.3 12.4 %collective-permute-start.21 = (s16[32,4224]{1,0:T(8,128)(2,1)S(1)}, s16[32,4224]{1,0:T(8,128)(2,1)S(1)}, u32[]{:S(2)}, u32[]{:S(2)}) collective-permute-start(s16[32,4224]{1,0:T(8,128)(2,1)S(1)} %collective-permute-done.12.rest_1_), channel_id=1, source_target_pairs={{0,8},{8,0},{16,24},{24,16},{32,40},{40,32},{48,56},{56,48},{64,72... | collective-permute-start | bytes 811016 | tf_op jit(solution)/shard_map/ppermute | solution.py:415
  80.1 7.7 %collective-permute-start.25 = (s16[32,4224]{1,0:T(8,128)(2,1)S(1)}, s16[32,4224]{1,0:T(8,128)(2,1)S(1)}, u32[]{:S(2)}, u32[]{:S(2)}) collective-permute-start(s16[32,4224]{1,0:T(8,128)(2,1)S(1)} %collective-permute-done.17.rest_5_), channel_id=1, source_target_pairs={{0,8},{8,0},{16,24},{24,16},{32,40},{40,32},{48,56},{56,48},{64,72... | collective-permute-start | bytes 811016 | tf_op jit(solution)/shard_map/ppermute | solution.py:415
  80.1 7.7 %collective-permute-start.26 = (s16[32,4224]{1,0:T(8,128)(2,1)S(1)}, s16[32,4224]{1,0:T(8,128)(2,1)S(1)}, u32[]{:S(2)}, u32[]{:S(2)}) collective-permute-start(s16[32,4224]{1,0:T(8,128)(2,1)S(1)} %collective-permute-done.18.rest_6_), channel_id=1, source_target_pairs={{0,8},{8,0},{16,24},{24,16},{32,40},{40,32},{48,56},{56,48},{64,72... | collective-permute-start | bytes 811016 | tf_op jit(solution)/shard_map/ppermute | solution.py:415
  80.6 7.2 %collective-permute-start.23 = (s16[32,4224]{1,0:T(8,128)(2,1)S(1)}, s16[32,4224]{1,0:T(8,128)(2,1)S(1)}, u32[]{:S(2)}, u32[]{:S(2)}) collective-permute-start(s16[32,4224]{1,0:T(8,128)(2,1)S(1)} %collective-permute-done.14.rest_3_), channel_id=1, source_target_pairs={{0,8},{8,0},{16,24},{24,16},{32,40},{40,32},{48,56},{56,48},{64,72... | collective-permute-start | bytes 811016 | tf_op jit(solution)/shard_map/ppermute | solution.py:415
  80.7 7.1 %collective-permute-start.27 = (s16[32,4224]{1,0:T(8,128)(2,1)S(1)}, s16[32,4224]{1,0:T(8,128)(2,1)S(1)}, u32[]{:S(2)}, u32[]{:S(2)}) collective-permute-start(s16[32,4224]{1,0:T(8,128)(2,1)S(1)} %collective-permute-done.19.rest_7_), channel_id=1, source_target_pairs={{0,8},{8,0},{16,24},{24,16},{32,40},{40,32},{48,56},{56,48},{64,72... | collective-permute-start | bytes 811016 | tf_op jit(solution)/shard_map/ppermute | solution.py:415

commit v2 on v1

--- a/solution.py
+++ b/solution.py
@@ -228,16 +228,17 @@
     )(near, far, places)
 
 
-def solve_kernel(
-    own_ref, sibling_ref, columns_ref, high_ref, low_ref, entries_ref, value, wanted, powers, rest_low, inverse
-):
+def solve_kernel(*refs):
+    parts = refs[:-9]
+    columns_ref, high_ref, low_ref, entries_ref, value, wanted, powers, rest_low, inverse = refs[-9:]
     order = entries_ref.shape[0]
     rows = columns_ref.shape[0]
     me = lax.axis_index("row")
     height = order // len(ENTRY_ORDER)
+    share = len(ENTRY_ORDER) // len(parts)
     for i, relative in enumerate(ENTRY_ORDER):
-        ref = own_ref if i < len(ENTRY_ORDER) // 2 else sibling_ref
-        at = (i % (len(ENTRY_ORDER) // 2)) * height
+        ref = parts[i // share]
+        at = (i % share) * height
         start = pl.multiple_of((me ^ relative) * height, height)
         entries_ref[pl.ds(start, height), :] = ref[at : at + height, :]
     row = lax.broadcasted_iota(jnp.int32, (order, order), 0)
@@ -332,12 +333,12 @@
         finish(solved)
 
 
-def solve(own, sibling, columns):
+def solve(parts, columns):
     rows, order = columns.shape
     return pl.pallas_call(
         solve_kernel,
         out_shape=(jax.ShapeDtypeStruct((rows, order), bf16),) * 2,
-        in_specs=[vmem_spec()] * 3,
+        in_specs=[vmem_spec()] * (len(parts) + 1),
         out_specs=(vmem_spec(), vmem_spec()),
         scratch_shapes=[
             VMEM((order, order), f32),
@@ -349,7 +350,7 @@
         ],
         name="solve",
         compiler_params=pltpu.CompilerParams(vmem_limit_bytes=24 * MIB),
-    )(own, sibling, columns)
+    )(*parts, columns)
 
 
 def update_kernel(weights_ref, high_ref, low_ref, *rest):
@@ -436,9 +437,11 @@
     entries, places = compact(near, far, height, order)
     entries = grow(entries, "row", Z_ONE)
     entries = grow(entries, "row", Z_TWO)
-    entries = grow(entries, "row", Y_ONE)
-    entries = grow(entries, "row", Y_THREE)
-    sibling = swap(entries, "row", CORE)
+    entries_one = swap(entries, "row", Y_ONE)
+    entries_three = swap(entries, "row", Y_THREE)
+    entries_two = swap(entries_one, "row", Y_THREE)
+    parts = [entries, entries_one, entries_three, entries_two]
+    parts = parts + [swap(e, "row", CORE) for e in parts]
 
     mine_near = grow(grow(mine, "col", Z_HALF), "col", X_ONE)
     mine_far = swap(mine_near, "col", X_THREE)
@@ -455,7 +458,7 @@
     panels = [even, even_one, even_three, even_two, odd, odd_three, odd_one, odd_two]
     panels = panels + [swap(p, "row", CORE) for p in panels]
 
-    high, low = solve(entries, sibling, columns)
+    high, low = solve(parts, columns)
     return update(weights, high, low, panels)
 
 

time: 93.8 us -> 88.9 us (0.948)
  starting transfers between devices: 54.6 us -> 46.5 us
  waiting for transfers between devices: 20.2 us -> 23.1 us
    ppermute x28 -> x32, starting transfers between devices: 54.6 us -> 46.5 us  [swap(): return lax.ppermute(value, axis, [(i, i ^ relative) for i in range(size)])]
    ppermute x28 -> x32, waiting for transfers between devices: 20.2 us -> 23.1 us  [swap(): return lax.ppermute(value, axis, [(i, i ^ relative) for i in range(size)])]
  transfers between devices with their start and end apart: 28 -> 32, of which waited for: 7 -> 9; matrix products, arithmetic and copies ran while one was open for 1% -> 1% of each run, Pallas kernels for 7% -> 8%
where the time goes in v2:
time: 88.9 us; the launch traced here: 88.7 us
  starting transfers between devices  46.5 us (52%)
  waiting for transfers between devices  23.1 us (26%)
  Pallas kernels  16.6 us (19%)
  local copies, waits for them, and re-layouts  1.32 us (1%)
  other arithmetic  1 us (1%)
    ppermute x32, starting transfers between devices, swap(): return lax.ppermute(value, axis, [(i, i ^ relative) for i in range(size)])  46.5 us
    ppermute x32, waiting for transfers between devices, swap(): return lax.ppermute(value, axis, [(i, i ^ relative) for i in range(size)])  23.1 us
    pallas_call x1, Pallas kernels, solve(): pl.pallas_call(solve_kernel, out_shape=(jax.ShapeDtypeStruct((rows, order...  6.12 us
    pallas_call x1, Pallas kernels, update(): pl.pallas_call(update_kernel, out_shape=jax.ShapeDtypeStruct((rows, width...  5.91 us
    pallas_call x1, Pallas kernels, prepare(): pl.pallas_call(prepare_kernel, out_shape=(jax.ShapeDtypeStruct((height, w...  3.32 us
  transfers between devices with their start and end apart: 32, of which 9 were waited for; matrix products, arithmetic and copies ran while one was open for 1% of the time, Pallas kernels for 8%

profile of v2, /device:TPU:1, one launch (start us, length us, event | category | flops | bytes accessed | tf_op | source)
XLA Modules:
  0.0 88.7 jit_solution(4196426117357473529)
XLA Ops:
  0.0 0.7 copy-done.1
  0.7 0.7 copy-done.2
  1.3 3.3 %prepare.1 = (s16[16,4224]{1,0:T(8,128)(2,1)}, bf16[64,128]{1,0:T(8,128)(2,1)S(1)}, bf16[256,128]{1,0:T(8,128)(2,1)S(1)}) custom-call(f32[8,4096]{1,0:T(8,128)} %first_hbm.1, f32[8,4096]{1,0:T(8,128)} %second_hbm.1, s32[1,64]{1,0:T(1,128)S(1)} %bitcast.2, s32[1,64]{1,0:T(1,128)S(1)} %bitcast.3, bf16[256,4096]{1,0:T(8,128)(2,1)} %weights_ref.1), custom_call_target="tpu_custom_call" | custom-call | tf_op jit(solution)/shard_map/prepare/pallas_call | solution.py:120
  4.6 7.8 %collective-permute-start = (bf16[64,128]{1,0:T(8,128)(2,1)S(1)}, bf16[64,128]{1,0:T(8,128)(2,1)S(1)}, u32[]{:S(2)}, u32[]{:S(2)}) collective-permute-start(bf16[64,128]{1,0:T(8,128)(2,1)S(1)} %get-tuple-element.12), channel_id=1, source_target_pairs={{0,4},{1,5},{2,6},{3,7},{4,0},{5,1},{6,2},{7,3},{8,12},{9,13},{10,... | collective-permute-start | bytes 49160 | tf_op jit(solution)/shard_map/ppermute | solution.py:416
  12.5 1.1 %collective-permute-done = bf16[64,128]{1,0:T(8,128)(2,1)S(1)} collective-permute-done((bf16[64,128]{1,0:T(8,128)(2,1)S(1)}, bf16[64,128]{1,0:T(8,128)(2,1)S(1)}, u32[]{:S(2)}, u32[]{:S(2)}) %collective-permute-start) | collective-permute-done | bytes 16416 | tf_op jit(solution)/shard_map/ppermute | solution.py:416
  13.6 1.2 %collective-permute-start.1 = (bf16[128,128]{1,0:T(8,128)(2,1)S(1)}, bf16[128,128]{1,0:T(8,128)(2,1)S(1)}, u32[]{:S(2)}, u32[]{:S(2)}) collective-permute-start(bf16[128,128]{1,0:T(8,128)(2,1)S(1)} %pad_maximum_fusion.5), channel_id=1, source_target_pairs={{0,1},{1,0},{2,3},{3,2},{4,5},{5,4},{6,7},{7,6},{8,9},{9,8},{10,11... | collective-permute-start | bytes 98312 | tf_op jit(solution)/shard_map/ppermute | solution.py:416
  14.8 1.6 %collective-permute-done.1 = bf16[128,128]{1,0:T(8,128)(2,1)S(1)} collective-permute-done((bf16[128,128]{1,0:T(8,128)(2,1)S(1)}, bf16[128,128]{1,0:T(8,128)(2,1)S(1)}, u32[]{:S(2)}, u32[]{:S(2)}) %collective-permute-start.1) | collective-permute-done | bytes 32800 | tf_op jit(solution)/shard_map/ppermute | solution.py:416
  16.4 2.5 %collective-permute-start.2 = (bf16[256,128]{1,0:T(8,128)(2,1)S(1)}, bf16[256,128]{1,0:T(8,128)(2,1)S(1)}, u32[]{:S(2)}, u32[]{:S(2)}) collective-permute-start(bf16[256,128]{1,0:T(8,128)(2,1)S(1)} %pad_maximum_fusion.3.near_ref), channel_id=1, source_target_pairs={{0,3},{1,2},{2,1},{3,0},{4,7},{5,6},{6,5},{7,4},{8,11},{9,10},{10,... | collective-permute-start | bytes 196616 | tf_op jit(solution)/shard_map/ppermute | solution.py:416
  18.8 5.4 %collective-permute-start.12 = (bf16[256,128]{1,0:T(8,128)(2,1)S(1)}, bf16[256,128]{1,0:T(8,128)(2,1)S(1)}, u32[]{:S(2)}, u32[]{:S(2)}) collective-permute-start(bf16[256,128]{1,0:T(8,128)(2,1)S(1)} %get-tuple-element.14), channel_id=1, source_target_pairs={{0,4},{1,5},{2,6},{3,7},{4,0},{5,1},{6,2},{7,3},{8,12},{9,13},{10,... | collective-permute-start | bytes 196616 | tf_op jit(solution)/shard_map/ppermute | solution.py:416
  24.2 1.6 %collective-permute-start.20 = (s16[16,4224]{1,0:T(8,128)(2,1)}, s16[16,4224]{1,0:T(8,128)(2,1)S(1)}, u32[]{:S(2)}, u32[]{:S(2)}) collective-permute-start(s16[16,4224]{1,0:T(8,128)(2,1)} %get-tuple-element.18), channel_id=1, source_target_pairs={{0,192},{8,200},{16,208},{24,216},{32,224},{40,232},{48,240},{56,2... | collective-permute-start | bytes 405512 | tf_op jit(solution)/shard_map/ppermute | solution.py:416
  26.1 1.6 %collective-permute-start.15 = (s16[16,4224]{1,0:T(8,128)(2,1)}, s16[16,4224]{1,0:T(8,128)(2,1)S(1)}, u32[]{:S(2)}, u32[]{:S(2)}) collective-permute-start(s16[16,4224]{1,0:T(8,128)(2,1)} %get-tuple-element.18), channel_id=1, source_target_pairs={{0,64},{8,72},{16,80},{24,88},{32,96},{40,104},{48,112},{56,120},{... | collective-permute-start | bytes 405512 | tf_op jit(solution)/shard_map/ppermute | solution.py:416
  28.5 7.3 %collective-permute-done.3 = f32[16,512]{1,0:T(8,128)S(1)} collective-permute-done((f32[16,512]{1,0:T(8,128)S(1)}, f32[16,512]{1,0:T(8,128)S(1)}, u32[]{:S(2)}, u32[]{:S(2)}) %collective-permute-start.3) | collective-permute-done | bytes 32800 | tf_op jit(solution)/shard_map/ppermute | solution.py:416
  35.8 1.7 %collective-permute-start.4 = (f32[32,512]{1,0:T(8,128)S(1)}, f32[32,512]{1,0:T(8,128)S(1)}, u32[]{:S(2)}, u32[]{:S(2)}) collective-permute-start(f32[32,512]{1,0:T(8,128)S(1)} %pad_maximum_fusion.4), channel_id=1, source_target_pairs={{0,128},{8,136},{16,144},{24,152},{32,160},{40,168},{48,176},{56,1... | collective-permute-start | bytes 196616 | tf_op jit(solution)/shard_map/ppermute | solution.py:416
  37.5 0.9 %pad_add_fusion.rest_0_ = s16[32,4224]{1,0:T(8,128)(2,1)S(1)} fusion(s16[16,4224]{1,0:T(8,128)(2,1)S(1)} %collective-permute-done.15, s16[16,4224]{1,0:T(8,128)(2,1)} %get-tuple-element.18), kind=kLoop, calls=%fused_computation | loop fusion | flops 135168 | bytes 540672 | tf_op jit(solution)/shard_map/concatenate | solution.py:424
  38.4 3.3 %collective-permute-start.24 = (s16[32,4224]{1,0:T(8,128)(2,1)S(1)}, s16[32,4224]{1,0:T(8,128)(2,1)S(1)}, u32[]{:S(2)}, u32[]{:S(2)}) collective-permute-start(s16[32,4224]{1,0:T(8,128)(2,1)S(1)} %pad_add_fusion.rest_0_), channel_id=1, source_target_pairs={{0,8},{8,0},{16,24},{24,16},{32,40},{40,32},{48,56},{56,48},{64,72... | collective-permute-start | bytes 811016 | tf_op jit(solution)/shard_map/ppermute | solution.py:416
  41.8 2.7 %collective-permute-start.17 = (s16[32,4224]{1,0:T(8,128)(2,1)S(1)}, s16[32,4224]{1,0:T(8,128)(2,1)S(1)}, u32[]{:S(2)}, u32[]{:S(2)}) collective-permute-start(s16[32,4224]{1,0:T(8,128)(2,1)S(1)} %pad_add_fusion.rest_0_), channel_id=1, source_target_pairs={{0,48},{8,56},{16,32},{24,40},{32,16},{40,24},{48,0},{56,8},{64,11... | collective-permute-start | bytes 811016 | tf_op jit(solution)/shard_map/ppermute | solution.py:416
  44.5 1.9 %collective-permute-start.8 = (f32[64,512]{1,0:T(8,128)S(1)}, f32[64,512]{1,0:T(8,128)S(1)}, u32[]{:S(2)}, u32[]{:S(2)}) collective-permute-start(f32[64,512]{1,0:T(8,128)S(1)} %pad_maximum_fusion.1.refs_0_), channel_id=1, source_target_pairs={{0,8},{8,0},{16,24},{24,16},{32,40},{40,32},{48,56},{56,48},{64,72... | collective-permute-start | bytes 393224 | tf_op jit(solution)/shard_map/ppermute | solution.py:416
  46.6 0.8 collective-permute-done.8.refs_4_
  47.4 0.7 collective-permute-start.16
  48.1 5.0 %collective-permute-done.6.refs_2_ = f32[64,512]{1,0:T(8,128)S(1)} collective-permute-done((f32[64,512]{1,0:T(8,128)S(1)}, f32[64,512]{1,0:T(8,128)S(1)}, u32[]{:S(2)}, u32[]{:S(2)}) %collective-permute-start.6) | collective-permute-done | bytes 131104 | tf_op jit(solution)/shard_map/ppermute | solution.py:416
  53.2 1.6 %collective-permute-start.28 = (s16[32,4224]{1,0:T(8,128)(2,1)S(1)}, s16[32,4224]{1,0:T(8,128)(2,1)S(1)}, u32[]{:S(2)}, u32[]{:S(2)}) collective-permute-start(s16[32,4224]{1,0:T(8,128)(2,1)S(1)} %pad_add_fusion.1.rest_4_), channel_id=1, source_target_pairs={{0,8},{8,0},{16,24},{24,16},{32,40},{40,32},{48,56},{56,48},{64,72... | collective-permute-start | bytes 811016 | tf_op jit(solution)/shard_map/ppermute | solution.py:416
  54.8 2.9 %collective-permute-start.21 = (s16[32,4224]{1,0:T(8,128)(2,1)S(1)}, s16[32,4224]{1,0:T(8,128)(2,1)S(1)}, u32[]{:S(2)}, u32[]{:S(2)}) collective-permute-start(s16[32,4224]{1,0:T(8,128)(2,1)S(1)} %pad_add_fusion.1.rest_4_), channel_id=1, source_target_pairs={{0,48},{8,56},{16,32},{24,40},{32,16},{40,24},{48,0},{56,8},{64,11... | collective-permute-start | bytes 811016 | tf_op jit(solution)/shard_map/ppermute | solution.py:416
  58.6 2.5 %collective-permute-start.18 = (s16[32,4224]{1,0:T(8,128)(2,1)S(1)}, s16[32,4224]{1,0:T(8,128)(2,1)S(1)}, u32[]{:S(2)}, u32[]{:S(2)}) collective-permute-start(s16[32,4224]{1,0:T(8,128)(2,1)S(1)} %collective-permute-done.16.rest_1_), channel_id=1, source_target_pairs={{0,48},{8,56},{16,32},{24,40},{32,16},{40,24},{48,0},{56,8},{64,11... | collective-permute-start | bytes 811016 | tf_op jit(solution)/shard_map/ppermute | solution.py:416
  61.1 3.1 %collective-permute-done.21.rest_5_ = s16[32,4224]{1,0:T(8,128)(2,1)S(1)} collective-permute-done((s16[32,4224]{1,0:T(8,128)(2,1)S(1)}, s16[32,4224]{1,0:T(8,128)(2,1)S(1)}, u32[]{:S(2)}, u32[]{:S(2)}) %collective-permute-start.21) | collective-permute-done | bytes 270368 | tf_op jit(solution)/shard_map/ppermute | solution.py:416
  64.9 1.6 %collective-permute-start.10 = (f32[64,512]{1,0:T(8,128)S(1)}, f32[64,512]{1,0:T(8,128)S(1)}, u32[]{:S(2)}, u32[]{:S(2)}) collective-permute-start(f32[64,512]{1,0:T(8,128)S(1)} %collective-permute-done.6.refs_2_), channel_id=1, source_target_pairs={{0,8},{8,0},{16,24},{24,16},{32,40},{40,32},{48,56},{56,48},{64,72... | collective-permute-start | bytes 393224 | tf_op jit(solution)/shard_map/ppermute | solution.py:416
  66.6 2.2 %collective-permute-start.7 = (f32[64,512]{1,0:T(8,128)S(1)}, f32[64,512]{1,0:T(8,128)S(1)}, u32[]{:S(2)}, u32[]{:S(2)}) collective-permute-start(f32[64,512]{1,0:T(8,128)S(1)} %collective-permute-done.5.refs_1_), channel_id=1, source_target_pairs={{0,48},{8,56},{16,32},{24,40},{32,16},{40,24},{48,0},{56,8},{64,11... | collective-permute-start | bytes 393224 | tf_op jit(solution)/shard_map/ppermute | solution.py:416
  69.2 2.9 %collective-permute-done.7.refs_3_ = f32[64,512]{1,0:T(8,128)S(1)} collective-permute-done((f32[64,512]{1,0:T(8,128)S(1)}, f32[64,512]{1,0:T(8,128)S(1)}, u32[]{:S(2)}, u32[]{:S(2)}) %collective-permute-start.7) | collective-permute-done | bytes 131104 | tf_op jit(solution)/shard_map/ppermute | solution.py:416
  72.1 1.8 %collective-permute-start.11 = (f32[64,512]{1,0:T(8,128)S(1)}, f32[64,512]{1,0:T(8,128)S(1)}, u32[]{:S(2)}, u32[]{:S(2)}) collective-permute-start(f32[64,512]{1,0:T(8,128)S(1)} %collective-permute-done.7.refs_3_), channel_id=1, source_target_pairs={{0,8},{8,0},{16,24},{24,16},{32,40},{40,32},{48,56},{56,48},{64,72... | collective-permute-start | bytes 393224 | tf_op jit(solution)/shard_map/ppermute | solution.py:416
  73.9 1.0 %collective-permute-done.11.refs_7_ = f32[64,512]{1,0:T(8,128)S(1)} collective-permute-done((f32[64,512]{1,0:T(8,128)S(1)}, f32[64,512]{1,0:T(8,128)S(1)}, u32[]{:S(2)}, u32[]{:S(2)}) %collective-permute-start.11) | collective-permute-done | bytes 131104 | tf_op jit(solution)/shard_map/ppermute | solution.py:416
  75.9 0.7 place.1.refs_8_
  76.6 6.1 %solve.1 = (bf16[256,512]{1,0:T(8,128)(2,1)S(1)}, bf16[256,512]{1,0:T(8,128)(2,1)S(1)}) custom-call(f32[64,512]{1,0:T(8,128)S(1)} %pad_maximum_fusion.1.refs_0_, f32[64,512]{1,0:T(8,128)S(1)} %collective-permute-done.5.refs_1_, f32[64,512]{1,0:T(8,128)S(1)} %collective-permute-done.6.refs_2_, f32[64,512]{1,0:T(8,128)S(1)} %collective-permute-done.7.refs_3_, ...), custom_call_target="tpu_custom_call" | custom-call | tf_op jit(solution)/shard_map/solve/pallas_call | solution.py:338
  82.8 5.9 %update.1 = bf16[256,4096]{1,0:T(8,128)(2,1)} custom-call(bf16[256,4096]{1,0:T(8,128)(2,1)S(1)} %copy-done, bf16[256,512]{1,0:T(8,128)(2,1)S(1)} %get-tuple-element.16.high_ref, bf16[256,512]{1,0:T(8,128)(2,1)S(1)} %get-tuple-element.17.low_ref, s16[32,4224]{1,0:T(8,128)(2,1)S(1)} %pad_add_fusion.rest_0_, ...), custom_call_target="tpu_custom_call" | custom-call | tf_op jit(solution)/shard_map/update/pallas_call | solution.py:397
  (51 shorter events, 4.3 us)
Async XLA Ops:
  4.6 8.9 %collective-permute-start = (bf16[64,128]{1,0:T(8,128)(2,1)S(1)}, bf16[64,128]{1,0:T(8,128)(2,1)S(1)}, u32[]{:S(2)}, u32[]{:S(2)}) collective-permute-start(bf16[64,128]{1,0:T(8,128)(2,1)S(1)} %get-tuple-element.12), channel_id=1, source_target_pairs={{0,4},{1,5},{2,6},{3,7},{4,0},{5,1},{6,2},{7,3},{8,12},{9,13},{10,... | collective-permute-start | bytes 49160 | tf_op jit(solution)/shard_map/ppermute | solution.py:416
  13.6 2.8 %collective-permute-start.1 = (bf16[128,128]{1,0:T(8,128)(2,1)S(1)}, bf16[128,128]{1,0:T(8,128)(2,1)S(1)}, u32[]{:S(2)}, u32[]{:S(2)}) collective-permute-start(bf16[128,128]{1,0:T(8,128)(2,1)S(1)} %pad_maximum_fusion.5), channel_id=1, source_target_pairs={{0,1},{1,0},{2,3},{3,2},{4,5},{5,4},{6,7},{7,6},{8,9},{9,8},{10,11... | collective-permute-start | bytes 98312 | tf_op jit(solution)/shard_map/ppermute | solution.py:416
  16.4 11.4 %collective-permute-start.2 = (bf16[256,128]{1,0:T(8,128)(2,1)S(1)}, bf16[256,128]{1,0:T(8,128)(2,1)S(1)}, u32[]{:S(2)}, u32[]{:S(2)}) collective-permute-start(bf16[256,128]{1,0:T(8,128)(2,1)S(1)} %pad_maximum_fusion.3.near_ref), channel_id=1, source_target_pairs={{0,3},{1,2},{2,1},{3,0},{4,7},{5,6},{6,5},{7,4},{8,11},{9,10},{10,... | collective-permute-start | bytes 196616 | tf_op jit(solution)/shard_map/ppermute | solution.py:416
  18.8 9.5 %collective-permute-start.12 = (bf16[256,128]{1,0:T(8,128)(2,1)S(1)}, bf16[256,128]{1,0:T(8,128)(2,1)S(1)}, u32[]{:S(2)}, u32[]{:S(2)}) collective-permute-start(bf16[256,128]{1,0:T(8,128)(2,1)S(1)} %get-tuple-element.14), channel_id=1, source_target_pairs={{0,4},{1,5},{2,6},{3,7},{4,0},{5,1},{6,2},{7,3},{8,12},{9,13},{10,... | collective-permute-start | bytes 196616 | tf_op jit(solution)/shard_map/ppermute | solution.py:416
  24.2 20.3 %collective-permute-start.20 = (s16[16,4224]{1,0:T(8,128)(2,1)}, s16[16,4224]{1,0:T(8,128)(2,1)S(1)}, u32[]{:S(2)}, u32[]{:S(2)}) collective-permute-start(s16[16,4224]{1,0:T(8,128)(2,1)} %get-tuple-element.18), channel_id=1, source_target_pairs={{0,192},{8,200},{16,208},{24,216},{32,224},{40,232},{48,240},{56,2... | collective-permute-start | bytes 405512 | tf_op jit(solution)/shard_map/ppermute | solution.py:416
  25.9 20.6 %collective-permute-start.19 = (s16[16,4224]{1,0:T(8,128)(2,1)}, s16[16,4224]{1,0:T(8,128)(2,1)S(1)}, u32[]{:S(2)}, u32[]{:S(2)}) collective-permute-start(s16[16,4224]{1,0:T(8,128)(2,1)} %get-tuple-element.18), channel_id=1, source_target_pairs={{0,128},{8,136},{16,144},{24,152},{32,160},{40,168},{48,176},{56,1... | collective-permute-start | bytes 405512 | tf_op jit(solution)/shard_map/ppermute | solution.py:416
  26.1 11.4 %collective-permute-start.15 = (s16[16,4224]{1,0:T(8,128)(2,1)}, s16[16,4224]{1,0:T(8,128)(2,1)S(1)}, u32[]{:S(2)}, u32[]{:S(2)}) collective-permute-start(s16[16,4224]{1,0:T(8,128)(2,1)} %get-tuple-element.18), channel_id=1, source_target_pairs={{0,64},{8,72},{16,80},{24,88},{32,96},{40,104},{48,112},{56,120},{... | collective-permute-start | bytes 405512 | tf_op jit(solution)/shard_map/ppermute | solution.py:416
  28.3 7.5 %collective-permute-start.3 = (f32[16,512]{1,0:T(8,128)S(1)}, f32[16,512]{1,0:T(8,128)S(1)}, u32[]{:S(2)}, u32[]{:S(2)}) collective-permute-start(f32[16,512]{1,0:T(8,128)S(1)} %get-tuple-element.13), channel_id=1, source_target_pairs={{0,64},{8,72},{16,80},{24,88},{32,96},{40,104},{48,112},{56,120},{... | collective-permute-start | bytes 98312 | tf_op jit(solution)/shard_map/ppermute | solution.py:416
  28.4 18.0 %collective-permute-start.13 = (bf16[512,128]{1,0:T(8,128)(2,1)S(1)}, bf16[512,128]{1,0:T(8,128)(2,1)S(1)}, u32[]{:S(2)}, u32[]{:S(2)}) collective-permute-start(bf16[512,128]{1,0:T(8,128)(2,1)S(1)} %pad_maximum_fusion.2), channel_id=1, source_target_pairs={{0,1},{1,0},{2,3},{3,2},{4,5},{5,4},{6,7},{7,6},{8,9},{9,8},{10,11... | collective-permute-start | bytes 393224 | tf_op jit(solution)/shard_map/ppermute | solution.py:416
  35.8 5.9 %collective-permute-start.4 = (f32[32,512]{1,0:T(8,128)S(1)}, f32[32,512]{1,0:T(8,128)S(1)}, u32[]{:S(2)}, u32[]{:S(2)}) collective-permute-start(f32[32,512]{1,0:T(8,128)S(1)} %pad_maximum_fusion.4), channel_id=1, source_target_pairs={{0,128},{8,136},{16,144},{24,152},{32,160},{40,168},{48,176},{56,1... | collective-permute-start | bytes 196616 | tf_op jit(solution)/shard_map/ppermute | solution.py:416
  38.4 16.3 %collective-permute-start.24 = (s16[32,4224]{1,0:T(8,128)(2,1)S(1)}, s16[32,4224]{1,0:T(8,128)(2,1)S(1)}, u32[]{:S(2)}, u32[]{:S(2)}) collective-permute-start(s16[32,4224]{1,0:T(8,128)(2,1)S(1)} %pad_add_fusion.rest_0_), channel_id=1, source_target_pairs={{0,8},{8,0},{16,24},{24,16},{32,40},{40,32},{48,56},{56,48},{64,72... | collective-permute-start | bytes 811016 | tf_op jit(solution)/shard_map/ppermute | solution.py:416
  41.8 16.0 %collective-permute-start.17 = (s16[32,4224]{1,0:T(8,128)(2,1)S(1)}, s16[32,4224]{1,0:T(8,128)(2,1)S(1)}, u32[]{:S(2)}, u32[]{:S(2)}) collective-permute-start(s16[32,4224]{1,0:T(8,128)(2,1)S(1)} %pad_add_fusion.rest_0_), channel_id=1, source_target_pairs={{0,48},{8,56},{16,32},{24,40},{32,16},{40,24},{48,0},{56,8},{64,11... | collective-permute-start | bytes 811016 | tf_op jit(solution)/shard_map/ppermute | solution.py:416
  44.5 2.9 %collective-permute-start.8 = (f32[64,512]{1,0:T(8,128)S(1)}, f32[64,512]{1,0:T(8,128)S(1)}, u32[]{:S(2)}, u32[]{:S(2)}) collective-permute-start(f32[64,512]{1,0:T(8,128)S(1)} %pad_maximum_fusion.1.refs_0_), channel_id=1, source_target_pairs={{0,8},{8,0},{16,24},{24,16},{32,40},{40,32},{48,56},{56,48},{64,72... | collective-permute-start | bytes 393224 | tf_op jit(solution)/shard_map/ppermute | solution.py:416
  46.4 6.7 %collective-permute-start.6 = (f32[64,512]{1,0:T(8,128)S(1)}, f32[64,512]{1,0:T(8,128)S(1)}, u32[]{:S(2)}, u32[]{:S(2)}) collective-permute-start(f32[64,512]{1,0:T(8,128)S(1)} %pad_maximum_fusion.1.refs_0_), channel_id=1, source_target_pairs={{0,48},{8,56},{16,32},{24,40},{32,16},{40,24},{48,0},{56,8},{64,11... | collective-permute-start | bytes 393224 | tf_op jit(solution)/shard_map/ppermute | solution.py:416
  46.4 8.3 %collective-permute-start.5 = (f32[64,512]{1,0:T(8,128)S(1)}, f32[64,512]{1,0:T(8,128)S(1)}, u32[]{:S(2)}, u32[]{:S(2)}) collective-permute-start(f32[64,512]{1,0:T(8,128)S(1)} %pad_maximum_fusion.1.refs_0_), channel_id=1, source_target_pairs={{0,16},{8,24},{16,0},{24,8},{32,48},{40,56},{48,32},{56,40},{64,80... | collective-permute-start | bytes 393224 | tf_op jit(solution)/shard_map/ppermute | solution.py:416
  47.4 10.6 %collective-permute-start.16 = (s16[32,4224]{1,0:T(8,128)(2,1)S(1)}, s16[32,4224]{1,0:T(8,128)(2,1)S(1)}, u32[]{:S(2)}, u32[]{:S(2)}) collective-permute-start(s16[32,4224]{1,0:T(8,128)(2,1)S(1)} %pad_add_fusion.rest_0_), channel_id=1, source_target_pairs={{0,16},{8,24},{16,0},{24,8},{32,48},{40,56},{48,32},{56,40},{64,80... | collective-permute-start | bytes 811016 | tf_op jit(solution)/shard_map/ppermute | solution.py:416
  53.2 5.5 %collective-permute-start.28 = (s16[32,4224]{1,0:T(8,128)(2,1)S(1)}, s16[32,4224]{1,0:T(8,128)(2,1)S(1)}, u32[]{:S(2)}, u32[]{:S(2)}) collective-permute-start(s16[32,4224]{1,0:T(8,128)(2,1)S(1)} %pad_add_fusion.1.rest_4_), channel_id=1, source_target_pairs={{0,8},{8,0},{16,24},{24,16},{32,40},{40,32},{48,56},{56,48},{64,72... | collective-permute-start | bytes 811016 | tf_op jit(solution)/shard_map/ppermute | solution.py:416
  54.7 10.1 %collective-permute-start.22 = (s16[32,4224]{1,0:T(8,128)(2,1)S(1)}, s16[32,4224]{1,0:T(8,128)(2,1)S(1)}, u32[]{:S(2)}, u32[]{:S(2)}) collective-permute-start(s16[32,4224]{1,0:T(8,128)(2,1)S(1)} %pad_add_fusion.1.rest_4_), channel_id=1, source_target_pairs={{0,16},{8,24},{16,0},{24,8},{32,48},{40,56},{48,32},{56,40},{64,80... | collective-permute-start | bytes 811016 | tf_op jit(solution)/shard_map/ppermute | solution.py:416
  54.8 9.5 %collective-permute-start.21 = (s16[32,4224]{1,0:T(8,128)(2,1)S(1)}, s16[32,4224]{1,0:T(8,128)(2,1)S(1)}, u32[]{:S(2)}, u32[]{:S(2)}) collective-permute-start(s16[32,4224]{1,0:T(8,128)(2,1)S(1)} %pad_add_fusion.1.rest_4_), channel_id=1, source_target_pairs={{0,48},{8,56},{16,32},{24,40},{32,16},{40,24},{48,0},{56,8},{64,11... | collective-permute-start | bytes 811016 | tf_op jit(solution)/shard_map/ppermute | solution.py:416
  57.7 8.9 %collective-permute-start.14 = (bf16[1024,128]{1,0:T(8,128)(2,1)S(1)}, bf16[1024,128]{1,0:T(8,128)(2,1)S(1)}, u32[]{:S(2)}, u32[]{:S(2)}) collective-permute-start(bf16[1024,128]{1,0:T(8,128)(2,1)S(1)} %pad_maximum_fusion.near_ref), channel_id=1, source_target_pairs={{0,3},{1,2},{2,1},{3,0},{4,7},{5,6},{6,5},{7,4},{8,11},{9,10},{10,... | collective-permute-start | bytes 786440 | tf_op jit(solution)/shard_map/ppermute | solution.py:416
  58.0 17.3 %collective-permute-start.26 = (s16[32,4224]{1,0:T(8,128)(2,1)S(1)}, s16[32,4224]{1,0:T(8,128)(2,1)S(1)}, u32[]{:S(2)}, u32[]{:S(2)}) collective-permute-start(s16[32,4224]{1,0:T(8,128)(2,1)S(1)} %collective-permute-done.17.rest_2_), channel_id=1, source_target_pairs={{0,8},{8,0},{16,24},{24,16},{32,40},{40,32},{48,56},{56,48},{64,72... | collective-permute-start | bytes 811016 | tf_op jit(solution)/shard_map/ppermute | solution.py:416
  58.6 16.8 %collective-permute-start.18 = (s16[32,4224]{1,0:T(8,128)(2,1)S(1)}, s16[32,4224]{1,0:T(8,128)(2,1)S(1)}, u32[]{:S(2)}, u32[]{:S(2)}) collective-permute-start(s16[32,4224]{1,0:T(8,128)(2,1)S(1)} %collective-permute-done.16.rest_1_), channel_id=1, source_target_pairs={{0,48},{8,56},{16,32},{24,40},{32,16},{40,24},{48,0},{56,8},{64,11... | collective-permute-start | bytes 811016 | tf_op jit(solution)/shard_map/ppermute | solution.py:416
  64.2 11.6 %collective-permute-start.23 = (s16[32,4224]{1,0:T(8,128)(2,1)S(1)}, s16[32,4224]{1,0:T(8,128)(2,1)S(1)}, u32[]{:S(2)}, u32[]{:S(2)}) collective-permute-start(s16[32,4224]{1,0:T(8,128)(2,1)S(1)} %collective-permute-done.21.rest_5_), channel_id=1, source_target_pairs={{0,16},{8,24},{16,0},{24,8},{32,48},{40,56},{48,32},{56,40},{64,80... | collective-permute-start | bytes 811016 | tf_op jit(solution)/shard_map/ppermute | solution.py:416
  64.9 4.0 %collective-permute-start.10 = (f32[64,512]{1,0:T(8,128)S(1)}, f32[64,512]{1,0:T(8,128)S(1)}, u32[]{:S(2)}, u32[]{:S(2)}) collective-permute-start(f32[64,512]{1,0:T(8,128)S(1)} %collective-permute-done.6.refs_2_), channel_id=1, source_target_pairs={{0,8},{8,0},{16,24},{24,16},{32,40},{40,32},{48,56},{56,48},{64,72... | collective-permute-start | bytes 393224 | tf_op jit(solution)/shard_map/ppermute | solution.py:416
  66.6 5.5 %collective-permute-start.7 = (f32[64,512]{1,0:T(8,128)S(1)}, f32[64,512]{1,0:T(8,128)S(1)}, u32[]{:S(2)}, u32[]{:S(2)}) collective-permute-start(f32[64,512]{1,0:T(8,128)S(1)} %collective-permute-done.5.refs_1_), channel_id=1, source_target_pairs={{0,48},{8,56},{16,32},{24,40},{32,16},{40,24},{48,0},{56,8},{64,11... | collective-permute-start | bytes 393224 | tf_op jit(solution)/shard_map/ppermute | solution.py:416
  68.8 5.1 %collective-permute-start.9 = (f32[64,512]{1,0:T(8,128)S(1)}, f32[64,512]{1,0:T(8,128)S(1)}, u32[]{:S(2)}, u32[]{:S(2)}) collective-permute-start(f32[64,512]{1,0:T(8,128)S(1)} %collective-permute-done.5.refs_1_), channel_id=1, source_target_pairs={{0,8},{8,0},{16,24},{24,16},{32,40},{40,32},{48,56},{56,48},{64,72... | collective-permute-start | bytes 393224 | tf_op jit(solution)/shard_map/ppermute | solution.py:416
  72.1 2.8 %collective-permute-start.11 = (f32[64,512]{1,0:T(8,128)S(1)}, f32[64,512]{1,0:T(8,128)S(1)}, u32[]{:S(2)}, u32[]{:S(2)}) collective-permute-start(f32[64,512]{1,0:T(8,128)S(1)} %collective-permute-done.7.refs_3_), channel_id=1, source_target_pairs={{0,8},{8,0},{16,24},{24,16},{32,40},{40,32},{48,56},{56,48},{64,72... | collective-permute-start | bytes 393224 | tf_op jit(solution)/shard_map/ppermute | solution.py:416
  73.9 8.9 %collective-permute-start.25 = (s16[32,4224]{1,0:T(8,128)(2,1)S(1)}, s16[32,4224]{1,0:T(8,128)(2,1)S(1)}, u32[]{:S(2)}, u32[]{:S(2)}) collective-permute-start(s16[32,4224]{1,0:T(8,128)(2,1)S(1)} %collective-permute-done.16.rest_1_), channel_id=1, source_target_pairs={{0,8},{8,0},{16,24},{24,16},{32,40},{40,32},{48,56},{56,48},{64,72... | collective-permute-start | bytes 811016 | tf_op jit(solution)/shard_map/ppermute | solution.py:416
  74.9 7.9 %collective-permute-start.29 = (s16[32,4224]{1,0:T(8,128)(2,1)S(1)}, s16[32,4224]{1,0:T(8,128)(2,1)S(1)}, u32[]{:S(2)}, u32[]{:S(2)}) collective-permute-start(s16[32,4224]{1,0:T(8,128)(2,1)S(1)} %collective-permute-done.21.rest_5_), channel_id=1, source_target_pairs={{0,8},{8,0},{16,24},{24,16},{32,40},{40,32},{48,56},{56,48},{64,72... | collective-permute-start | bytes 811016 | tf_op jit(solution)/shard_map/ppermute | solution.py:416
  75.3 7.5 %collective-permute-start.30 = (s16[32,4224]{1,0:T(8,128)(2,1)S(1)}, s16[32,4224]{1,0:T(8,128)(2,1)S(1)}, u32[]{:S(2)}, u32[]{:S(2)}) collective-permute-start(s16[32,4224]{1,0:T(8,128)(2,1)S(1)} %collective-permute-done.22.rest_6_), channel_id=1, source_target_pairs={{0,8},{8,0},{16,24},{24,16},{32,40},{40,32},{48,56},{56,48},{64,72... | collective-permute-start | bytes 811016 | tf_op jit(solution)/shard_map/ppermute | solution.py:416
  75.4 7.4 %collective-permute-start.27 = (s16[32,4224]{1,0:T(8,128)(2,1)S(1)}, s16[32,4224]{1,0:T(8,128)(2,1)S(1)}, u32[]{:S(2)}, u32[]{:S(2)}) collective-permute-start(s16[32,4224]{1,0:T(8,128)(2,1)S(1)} %collective-permute-done.18.rest_3_), channel_id=1, source_target_pairs={{0,8},{8,0},{16,24},{24,16},{32,40},{40,32},{48,56},{56,48},{64,72... | collective-permute-start | bytes 811016 | tf_op jit(solution)/shard_map/ppermute | solution.py:416
  75.8 7.0 %collective-permute-start.31 = (s16[32,4224]{1,0:T(8,128)(2,1)S(1)}, s16[32,4224]{1,0:T(8,128)(2,1)S(1)}, u32[]{:S(2)}, u32[]{:S(2)}) collective-permute-start(s16[32,4224]{1,0:T(8,128)(2,1)S(1)} %collective-permute-done.23.rest_7_), channel_id=1, source_target_pairs={{0,8},{8,0},{16,24},{24,16},{32,40},{40,32},{48,56},{56,48},{64,72... | collective-permute-start | bytes 811016 | tf_op jit(solution)/shard_map/ppermute | solution.py:416
  (3 other events, 55.8 us)
